TPU v7x, 256 devices: a whole 4x4x8 slice. The times are simulated.
256 devices in a mesh: leaf: 4 (over x), row: 64 (over y, z, core).
Axes of the slice: x: 4, y: 4, z: 8, core: 2. Of those that a mesh axis runs over, the one named last changes fastest.
Arguments:
- right_side: bfloat16 [4, 256, 256, 512], P('leaf', 'row'), may hold values from -6 to 6
- panels: bfloat16 [4, 4, 256, 512, 512], P(None, 'leaf', 'row'), may hold values from -0.1875 to 0.1875
- tile_counts: int32 [4, 4, 256], P(None, 'leaf', 'row'), may hold values from 0 to 512, as said below
- diag_leaf: bfloat16 [4, 512, 512], P('leaf')
- diag_pair: bfloat16 [2, 512, 512], replicated
- diag_root: bfloat16 [2, 512, 512], replicated
- sup_rows: int32 [4], replicated, may hold values from 0 to 255, as said below
Outputs:
- solution: bfloat16 [4, 4, 256, 512], P(None, 'leaf')
- updated_side: bfloat16 [256, 256, 512], P('row')
Inputs may be any that keep to these rules, and one draw needn't show every extreme that they name: `sup_rows`: 4 distinct block rows, one a level. `tile_counts`: 0 marks a tile with no valid columns.
All inputs are finite; a program needn't handle non-finite values.
Results may differ from a plain program's by a relative error of at most 0.0062.
Values may be sent and summed in bfloat16 or wider, within the bound.
A program may use at most 128 MiB of HBM per device.

v0:
```python
import jax
import jax.numpy as jnp
from jax import lax
from jax.sharding import PartitionSpec as P


def swapped(shard, axis, apart):
    return lax.ppermute(shard, axis, [(i, i ^ 1 << apart) for i in range(lax.axis_size(axis))])


def picked(shard, axis, root):
    return lax.dynamic_index_in_dim(lax.all_gather(shard, axis), root, 0, keepdims=False)


def cut_along(shard, dim, size):
    lengths = shard.shape
    parts = shard.reshape(*lengths[:dim], size, lengths[dim] // size, *lengths[dim + 1 :])
    return jnp.moveaxis(parts, dim, 0)


def sum_at_owner(shard, axis, dim):
    parts = cut_along(shard, dim, lax.axis_size(axis))
    arrived = lax.all_to_all(parts, axis, split_axis=0, concat_axis=0, tiled=True)
    return arrived.sum(axis=0)


def from_everyone(shard, axis):
    copies = jnp.broadcast_to(shard, (lax.axis_size(axis), *shard.shape))
    return lax.all_to_all(copies, axis, split_axis=0, concat_axis=0, tiled=True)


def laid_out(parts, dim):
    lengths = list(parts.shape[1:])
    lengths[dim] *= parts.shape[0]
    return jnp.moveaxis(parts, 0, dim).reshape(lengths)


def collect(shard, axis, dim):
    parts = from_everyone(shard, axis)
    return laid_out(parts, dim)


def merge_pairs(partial_result):
    merged = partial_result + swapped(partial_result, "leaf", 0)
    return merged


def solve_owned(merged, inverse, is_owner):

    def compute(values):
        return jnp.dot(
            values.astype(jnp.bfloat16), inverse, preferred_element_type=jnp.float32
        ).astype(jnp.bfloat16)

    def nothing(values):
        return jnp.zeros(values.shape, jnp.bfloat16)

    return lax.cond(is_owner, compute, nothing, merged)


def publish(current_solved, owner_row):
    return picked(current_solved, "row", owner_row)


def on_device(right_side, panels, tile_counts, diag_leaf, diag_pair, diag_root, sup_rows):
    leaf_position = lax.axis_index("leaf")
    row_index = lax.axis_index("row")
    levels = panels.shape[0]
    rows_here = panels.shape[2]
    tile_width = panels.shape[3]
    share_parts = right_side[0].astype(jnp.float32)
    totals = jnp.zeros(share_parts.shape, jnp.float32)
    tile_ids = row_index * rows_here + jnp.arange(rows_here, dtype=jnp.int32)
    columns = jnp.arange(tile_width, dtype=jnp.int32)
    solved = []
    for panel_height in range(levels):
        target_row = sup_rows[panel_height]
        owner_row = target_row // rows_here
        local_tile = target_row % rows_here
        is_owner = owner_row == row_index
        partial_result = lax.dynamic_index_in_dim(
            share_parts, local_tile, 0, keepdims=False
        ) - lax.dynamic_index_in_dim(totals, local_tile, 0, keepdims=False)
        if panel_height == 0:
            current_solved = publish(solve_owned(partial_result, diag_leaf[0], is_owner), owner_row)
        elif panel_height == 1:
            inverse = lax.dynamic_index_in_dim(diag_pair, leaf_position // 2, 0, keepdims=False)
            current_solved = publish(
                solve_owned(merge_pairs(partial_result), inverse, is_owner), owner_row
            )
        else:
            inverse = diag_root[panel_height - 2]
            piece_rhs = sum_at_owner(partial_result, "leaf", 0)
            slice_solved = publish(solve_owned(piece_rhs, inverse, is_owner), owner_row)
            current_solved = collect(slice_solved, "leaf", 0)
        solved.append(current_solved)
        structure = jnp.logical_not(
            jnp.any(tile_ids[:, None] == sup_rows[: panel_height + 1][None, :], axis=1)
        )
        col_mask = (
            (columns[None, :] < tile_counts[panel_height, 0][:, None]) & structure[:, None]
        ).astype(jnp.float32)
        update_term = jnp.einsum(
            "pi,bis->bps",
            current_solved,
            panels[panel_height, 0],
            preferred_element_type=jnp.float32,
        )
        totals = totals + update_term * col_mask[:, None, :]
    solution = jnp.stack(solved)[:, None]
    updated_side = lax.psum(share_parts - totals, "leaf").astype(jnp.bfloat16)
    return (solution, updated_side)


def solution(mesh):
    placed = (
        P("leaf", "row", None, None),
        P(None, "leaf", "row", None, None),
        P(None, "leaf", "row"),
        P("leaf", None, None),
        P(),
        P(),
        P(),
    )
    return jax.shard_map(
        on_device,
        mesh=mesh,
        in_specs=placed,
        out_specs=(P(None, "leaf", None, None), P("row", None, None)),
        check_vma=False,
    )
```

profile of v0, /device:TPU:1, one launch (start us, length us, event | category | flops | bytes accessed | tf_op | source)
XLA Modules:
  0.0 497.2 jit_solution(1703785792131386626)
XLA Ops:
  7.2 1.4 fusion.45
  14.1 2.8 convert_element_type.85
  17.7 98.1 %all-gather.9.cloned.1.call-done = bf16[16384,512]{1,0:T(8,128)(2,1)} async-done(((bf16[256,512]{1,0:T(8,128)(2,1)}), bf16[16384,512]{1,0:T(8,128)(2,1)}) %all-gather.9.cloned.1.call-update) | async-done | bytes 16777232 | tf_op jit(solution)/shard_map/all_gather | solution.py:12
  115.8 1.0 constant_dynamic-slice_fusion.1
  116.7 2.3 fusion.29
  119.1 1.1 fusion.34
  120.2 1.3 collective-permute-start
  122.1 11.4 %collective-permute-done = f32[256,512]{1,0:T(8,128)S(1)} collective-permute-done((f32[256,512]{1,0:T(8,128)S(1)}, f32[256,512]{1,0:T(8,128)S(1)}, u32[]{:S(2)}, u32[]{:S(2)}) %collective-permute-start) | collective-permute-done | bytes 524320 | tf_op jit(solution)/shard_map/ppermute | solution.py:8
  136.5 95.0 %all-gather.11.cloned.1.call-done = bf16[16384,512]{1,0:T(8,128)(2,1)} async-done(((bf16[256,512]{1,0:T(8,128)(2,1)}), bf16[16384,512]{1,0:T(8,128)(2,1)}) %all-gather.11.cloned.1.call-update) | async-done | bytes 16777232 | tf_op jit(solution)/shard_map/all_gather | solution.py:12
  231.5 1.0 constant_dynamic-slice_fusion
  232.5 2.4 multiply_add_fusion.1
  234.9 1.3 copy-done
  236.3 2.0 bitcast_subtract_fusion.2
  238.3 4.0 all-to-all-start
  242.9 8.4 %all-to-all-done = f32[4,64,512]{2,1,0:T(8,128)S(1)} async-done(((f32[4,64,512]{2,1,0:T(8,128)}), f32[4,64,512]{2,1,0:T(8,128)S(1)}, u32[]{:S(2)}, u32[]{:S(2)}) %all-to-all-start) | async-done | bytes 524320 | tf_op jit(solution)/shard_map/all_to_all | solution.py:23
  254.1 73.6 %all-gather.13.cloned.1.call-done = bf16[4096,512]{1,0:T(8,128)(2,1)} async-done(((bf16[64,512]{1,0:T(8,128)(2,1)}), bf16[4096,512]{1,0:T(8,128)(2,1)}) %all-gather.13.cloned.1.call-update) | async-done | bytes 4194320 | tf_op jit(solution)/shard_map/all_gather | solution.py:12
  327.7 0.8 dynamic-slice_bitcast_fusion.1
  328.5 0.7 broadcast_in_dim.6
  329.2 4.0 all-to-all-start.1
  333.3 5.8 %all-to-all-done.1 = bf16[4,64,512]{2,1,0:T(8,128)(2,1)S(1)} async-done(((bf16[4,64,512]{2,1,0:T(8,128)(2,1)}), bf16[4,64,512]{2,1,0:T(8,128)(2,1)S(1)}, u32[]{:S(2)}, u32[]{:S(2)}) %all-to-all-start.1) | async-done | bytes 262176 | tf_op jit(solution)/shard_map/all_to_all | solution.py:29
  339.1 3.0 multiply_add_fusion
  342.2 1.9 bitcast_subtract_fusion.1
  344.1 4.3 all-to-all-start.2
  349.1 6.9 %all-to-all-done.2 = f32[4,64,512]{2,1,0:T(8,128)} async-done(((f32[4,64,512]{2,1,0:T(8,128)}), f32[4,64,512]{2,1,0:T(8,128)}, u32[]{:S(2)}, u32[]{:S(2)}) %all-to-all-start.2) | async-done | bytes 524320 | tf_op jit(solution)/shard_map/all_to_all | solution.py:23
  356.9 76.9 %all-gather.15.cloned.1.call-done = bf16[4096,512]{1,0:T(8,128)(2,1)} async-done(((bf16[64,512]{1,0:T(8,128)(2,1)}), bf16[4096,512]{1,0:T(8,128)(2,1)}) %all-gather.15.cloned.1.call-update) | async-done | bytes 4194320 | tf_op jit(solution)/shard_map/all_gather | solution.py:12
  433.8 0.8 dynamic-slice_bitcast_fusion
  434.6 0.7 broadcast_in_dim.7
  435.4 4.0 all-to-all-start.3
  439.5 5.9 %all-to-all-done.3 = bf16[4,64,512]{2,1,0:T(8,128)(2,1)} async-done(((bf16[4,64,512]{2,1,0:T(8,128)(2,1)}), bf16[4,64,512]{2,1,0:T(8,128)(2,1)}, u32[]{:S(2)}, u32[]{:S(2)}) %all-to-all-start.3) | async-done | bytes 262176 | tf_op jit(solution)/shard_map/all_to_all | solution.py:29
  445.4 3.7 bitcast_subtract_fusion
  449.2 39.5 %all-reduce.1 = bf16[4,256,512]{2,1,0:T(8,128)(2,1)} all-reduce(f32[4,256,512]{2,1,0:T(8,128)} %bitcast_subtract_fusion), channel_id=1, replica_groups=mesh['leaf'=4,'row'=64] {'leaf'}, use_global_device_ids=true, to_apply=%region_13.14 | all-reduce | flops 524288 | bytes 3145728 | tf_op jit(solution)/shard_map/psum | solution.py:111
  488.6 2.1 maximum_bitcast_fusion
  (54 shorter events, 4.6 us)
Async XLA Ops:
  7.2 108.6 %all-gather.9.cloned.1.call-start = ((), (), s32[]{:S(2)}) async-start(), calls=%async_computation.4 | async-start | bytes 17039360 | tf_op jit(solution)/shard_map/all_gather | solution.py:12
  11.4 6.2 %copy-start.13 = (s32[4,1,4]{2,1,0:T(1,128)S(1)}, s32[4,1,4]{2,1,0:T(1,128)}, u32[]{:S(2)}) copy-start(s32[4,1,4]{2,1,0:T(1,128)} %param.17) | copy-start | bytes 196
  11.4 0.7 copy-start.7
  12.2 219.3 %all-gather.11.cloned.1.call-start = ((), (), s32[]{:S(2)}) async-start(), calls=%async_computation.5 | async-start | bytes 17039360 | tf_op jit(solution)/shard_map/all_gather | solution.py:12
  119.1 17.2 %copy-start.12 = (s32[4]{0:T(128)S(1)}, s32[4]{0:T(128)}, u32[]{:S(2)}) copy-start(s32[4]{0:T(128)} %param.21) | copy-start | bytes 52
  120.2 13.3 %collective-permute-start = (f32[256,512]{1,0:T(8,128)S(1)}, f32[256,512]{1,0:T(8,128)S(1)}, u32[]{:S(2)}, u32[]{:S(2)}) collective-permute-start(f32[256,512]{1,0:T(8,128)S(1)} %fusion.34), channel_id=1, source_target_pairs={{0,64},{64,0},{128,192},{192,128},{1,65},{65,1},{129,193},{193,129... | collective-permute-start | bytes 1572872 | tf_op jit(solution)/shard_map/ppermute | solution.py:8
  133.5 0.7 copy-start.8
  232.5 2.4 copy-start.2
  234.9 1.4 copy-start
  236.3 15.0 %copy-start.6 = (bf16[2,512,512]{2,1,0:T(8,128)(2,1)S(1)}, bf16[2,512,512]{2,1,0:T(8,128)(2,1)}, u32[]{:S(2)}) copy-start(bf16[2,512,512]{2,1,0:T(8,128)(2,1)} %param.20) | copy-start | bytes 3145732
  238.3 13.0 %all-to-all-start = ((f32[4,64,512]{2,1,0:T(8,128)}), f32[4,64,512]{2,1,0:T(8,128)S(1)}, u32[]{:S(2)}, u32[]{:S(2)}) async-start(f32[4,64,512]{2,1,0:T(8,128)} %bitcast.23), calls=%async_computation | async-start | bytes 1048576 | tf_op jit(solution)/shard_map/all_to_all | solution.py:23
  242.3 85.4 %all-gather.13.cloned.1.call-start = ((), (), s32[]{:S(2)}) async-start(), calls=%async_computation.6 | async-start | bytes 4259840 | tf_op jit(solution)/shard_map/all_gather | solution.py:12
  251.3 0.6 copy-start.10
  329.2 9.9 %all-to-all-start.1 = ((bf16[4,64,512]{2,1,0:T(8,128)(2,1)}), bf16[4,64,512]{2,1,0:T(8,128)(2,1)S(1)}, u32[]{:S(2)}, u32[]{:S(2)}) async-start(bf16[4,64,512]{2,1,0:T(8,128)(2,1)} %broadcast_in_dim.6), calls=%async_computation.1 | async-start | bytes 524288 | tf_op jit(solution)/shard_map/all_to_all | solution.py:29
  339.1 3.0 copy-start.4
  344.1 101.3 %copy-start.1 = (bf16[1,4,256,512]{3,2,1,0:T(8,128)(2,1)S(1)}, bf16[1,4,256,512]{3,2,1,0:T(8,128)(2,1)}, u32[]{:S(2)}) copy-start(bf16[1,4,256,512]{3,2,1,0:T(8,128)(2,1)} %param.15) | copy-start | bytes 3145732
  344.1 11.9 %all-to-all-start.2 = ((f32[4,64,512]{2,1,0:T(8,128)}), f32[4,64,512]{2,1,0:T(8,128)}, u32[]{:S(2)}, u32[]{:S(2)}) async-start(f32[4,64,512]{2,1,0:T(8,128)} %bitcast.107), calls=%async_computation.2 | async-start | bytes 1048576 | tf_op jit(solution)/shard_map/all_to_all | solution.py:23
  348.4 85.4 %all-gather.15.cloned.1.call-start = ((), (), s32[]{:S(2)}) async-start(), calls=%async_computation.7 | async-start | bytes 4259840 | tf_op jit(solution)/shard_map/all_gather | solution.py:12
  356.0 0.6 copy-start.11
  435.4 10.1 %all-to-all-start.3 = ((bf16[4,64,512]{2,1,0:T(8,128)(2,1)}), bf16[4,64,512]{2,1,0:T(8,128)(2,1)}, u32[]{:S(2)}, u32[]{:S(2)}) async-start(bf16[4,64,512]{2,1,0:T(8,128)(2,1)} %broadcast_in_dim.7), calls=%async_computation.3 | async-start | bytes 524288 | tf_op jit(solution)/shard_map/all_to_all | solution.py:29
  449.2 39.5 %copy-start.3 = (bf16[1,256,512]{2,1,0:T(8,128)(2,1)S(1)}, bf16[1,256,512]{2,1,0:T(8,128)(2,1)}, u32[]{:S(2)}) copy-start(bf16[1,256,512]{2,1,0:T(8,128)(2,1)} %copy-done.2) | copy-start | bytes 786436
  449.2 39.5 %copy-start.5 = (bf16[4,64,512]{2,1,0:T(8,128)(2,1)S(1)}, bf16[4,64,512]{2,1,0:T(8,128)(2,1)}, u32[]{:S(2)}) copy-start(bf16[4,64,512]{2,1,0:T(8,128)(2,1)} %copy-done.4) | copy-start | bytes 786436
Sparse Core Ops, SparseCore 0:
  12.3 103.4 all-gather.8
  134.4 97.0 all-gather.10
  252.1 75.5 all-gather.12
  356.8 76.9 all-gather.14
where the time goes:
time: 500 us; the launch traced here: 497 us
  waiting for transfers between devices  382 us (76%)
  blocking collectives  39.5 us (8%)
  between operations  24.4 us (5%)
  starting transfers between devices  17.6 us (4%)
  other arithmetic  11.5 us (2%)
  matrix products  11.5 us (2%)
  local copies, waits for them, and re-layouts  10.6 us (2%)
    all_gather x4, waiting for transfers between devices, picked(): lax.all_gather(shard, axis)  344 us
    psum x1, blocking collectives, on_device(): updated_side = lax.psum(share_parts - totals, 'leaf').astype(jnp.bfloat16)  39.5 us
    all_to_all x2, waiting for transfers between devices, sum_at_owner(): lax.all_to_all(parts, axis, split_axis=0, concat_axis=0, tiled=True)  15.3 us
    all_to_all x2, waiting for transfers between devices, from_everyone(): return lax.all_to_all(copies, axis, split_axis=0, concat_axis=0, tiled=True)  11.8 us
    dot_general x4, matrix products, on_device(): jnp.einsum('pi,bis->bps', current_solved, panels[panel_height, 0], prefer...  11.5 us
    ppermute x1, waiting for transfers between devices, swapped(): lax.ppermute(shard, axis, [(i, i ^ 1 << apart) for i in range(lax.axis_si...  11.4 us
  transfers between devices with their start and end apart: 9, of which 9 were waited for; matrix products, arithmetic and copies ran while one was open for 1% of the time, Pallas kernels for 0%

commit v1 on v0

v1 whole, which is shorter than its diff:
```python
import functools

import jax
import jax.numpy as jnp
from jax import lax
from jax.experimental import pallas as pl
from jax.experimental.pallas import tpu as pltpu
from jax.sharding import PartitionSpec as P

MESH = pl.DeviceIdType.MESH
F32, BF16 = jnp.float32, jnp.bfloat16
ROUNDS = ((0,), (1,), (2,), (3,))
GRIDS = {64: (4, 8, 2), 8: (2, 2, 2)}
SEMS = 96


def kernel(grid, n_leaf, sup, cnt, rs_h, pan_h, dl_h, dp_h, dr_h, sol_o, upd_o, *scratch):
    ny, nz, nc = grid
    (rs, pan, dl, dp, dr, held, qacc, sol, base, xr, fin, rest, sem) = scratch
    levels, (tiles, wide, _) = len(pan), pan[0].shape
    rhs = rs.shape[1]
    low = wide // ny
    x, r = lax.axis_index("leaf"), lax.axis_index("row")
    y, z, c = r // (nz * nc), (r // nc) % nz, r % nc
    used = [0]
    drains = []

    def device(x_, y_, z_, c_):
        return (x_, (y_ * nz + z_) * nc + c_)

    def fresh():
        used[0] += 1
        assert used[0] <= SEMS
        return sem.at[used[0] - 1]

    def fetch(src, dst):
        copy = pltpu.make_async_copy(src, dst, fresh())
        copy.start()
        return copy

    def exchange(copies, whole):
        out, got = fresh(), fresh()
        for src, dst, dev in copies:
            pltpu.make_async_remote_copy(
                src_ref=src, dst_ref=dst, send_sem=out, recv_sem=got, device_id=dev, device_id_type=MESH
            ).start()
        drains.append(pltpu.make_async_copy(whole, whole, out))
        return pltpu.make_async_copy(whole, whole, got)

    ready = {"rs": fetch(rs_h.at[0], rs), "d0": fetch(dl_h, dl)}
    ready["p0"] = fetch(pan_h.at[0, 0], pan[0])
    ready["d1"] = fetch(dp_h, dp)
    ready["p1"] = fetch(pan_h.at[1, 0], pan[1])
    ready["d2"] = fetch(dr_h, dr)
    ready["p2"] = fetch(pan_h.at[2, 0], pan[2])
    ready["p3"] = fetch(pan_h.at[3, 0], pan[3])
    waited = set()

    def need(name):
        if name not in waited:
            waited.add(name)
            ready[name].wait()

    barrier = pltpu.get_barrier_semaphore()
    peers = [device(x, y, z, 1 - c)]
    peers += [device(x, y, (z + k) % nz, c) for k in range(1, nz)]
    peers += [device(x ^ i, (y + j) % ny, z, c) for i in range(n_leaf) for j in range(ny) if i or j]
    for dev in peers:
        pl.semaphore_signal(barrier, inc=1, device_id=dev, device_id_type=MESH)
    pl.semaphore_wait(barrier, len(peers))

    owner = [jnp.where(lax.div(sup[m], tiles) == r, 1.0, 0.0).astype(F32) for m in range(levels)]
    local = [lax.rem(sup[m], tiles) for m in range(levels)]
    columns = lax.broadcasted_iota(jnp.int32, (1, wide), 1)

    def product(level, tile, count):
        done = sol[level].reshape(rhs, wide)
        term = jnp.dot(done, pan[level][tile], preferred_element_type=F32)
        return jnp.where(columns < count, term, 0.0)

    def bulk(level):
        def one(tile, carry):
            count = cnt[level, 0, tile]
            for m in range(level + 1):
                count = jnp.where(sup[m] == r * tiles + tile, 0, count)
            term = product(level, tile, count)
            before = rs[tile].astype(F32) if level == 0 else held[tile]
            held[tile] = before - term
            return carry

        lax.fori_loop(0, tiles, one, 0)

    inverses = [("d0", lambda: dl[0]), ("d1", lambda: dp[x // 2]), ("d2", lambda: dr[0]), ("d2", lambda: dr[1])]
    late = []
    for number, group in enumerate(ROUNDS):
        qs, qr, zs, zr, ys, yr = rest[number][:6]
        size = len(group)
        need("rs")
        for i, m in enumerate(group):
            part = rs[local[m]].astype(F32)
            if number:
                part = part - qacc[m]
            part = (part * owner[m]).astype(BF16)
            for half in range(nc):
                qs[half, i] = part[half * (rhs // nc) : (half + 1) * (rhs // nc)]
        exchange([(qs.at[1 - c], qr, device(x, y, z, 1 - c))], qr).wait()
        for i in range(size):
            both = qs[c, i].astype(F32) + qr[i].astype(F32)
            zs[:, i] = both.astype(BF16).reshape(nz, rhs // nc // nz, wide)
        arrival = exchange(
            [(zs.at[(z + k) % nz], zr.at[k - 1], device(x, y, (z + k) % nz, c)) for k in range(1, nz)], zr
        )
        for level in late:
            bulk(level)
        late = []
        arrival.wait()
        rows = zs[z].astype(F32)
        for k in range(nz - 1):
            rows = rows + zr[k].astype(F32)
        rows = rows.astype(BF16)
        for k in range(ny):
            ys[k] = rows[:, :, k * low : (k + 1) * low]
        exchange(
            [(ys.at[(y + k) % ny], yr.at[k - 1], device(x, (y + k) % ny, z, c)) for k in range(1, ny)], yr
        ).wait()
        piece = ys[y].astype(F32)
        for k in range(ny - 1):
            piece = piece + yr[k].astype(F32)
        spreads = []
        for i, m in enumerate(group):
            n = (1, 2, n_leaf, n_leaf)[m]
            cs, cr = rest[number][6 + i]
            own = (x % n) * ny + y
            cs[...] = piece[i]
            cr[own] = piece[i]
            exchange(
                [
                    (cs, cr.at[own], device(x ^ a, (y + b) % ny, z, c))
                    for a in range(n)
                    for b in range(ny)
                    if a or b
                ],
                cr.at[pl.ds(0, n * ny - 1)],
            ).wait()
            merged = []
            for k in range(ny):
                total = cr[k]
                for a in range(1, n):
                    total = total + cr[a * ny + k]
                merged.append(total.astype(BF16))
            merged = jnp.concatenate(merged, axis=1)
            name, inverse = inverses[m]
            need(name)
            sol[m, c, z] = jnp.dot(merged, inverse(), preferred_element_type=F32).astype(BF16)
            spreads.append(
                exchange(
                    [
                        (sol.at[m, c, z], sol.at[m, c, z], device(x, y, (z + k) % nz, c))
                        for k in range(1, nz)
                    ],
                    sol.at[m, c, pl.ds(0, nz - 1)],
                )
            )
        for m, spread in zip(group, spreads):
            spread.wait()
            exchange([(sol.at[m, c], sol.at[m, c], device(x, y, z, 1 - c))], sol.at[m, c]).wait()
            drains.append(fetch(sol.at[m], sol_o.at[m]))
        for m in group:
            need(f"p{m}")
            later = [k for rest_group in ROUNDS[number + 1 :] for k in rest_group]
            for k in later:
                term = product(m, local[k], cnt[m, 0, local[k]])
                qacc[k] = term if m == 0 else qacc[k] + term
        late = list(group)

    for level in late:
        bulk(level)
    for tile in range(tiles):
        base[tile] = held[tile].astype(BF16)
    exchange([(base.at[x ^ k], xr.at[k - 1], device(x ^ k, y, z, c)) for k in range(1, n_leaf)], xr).wait()
    total = held[x]
    for k in range(n_leaf - 1):
        total = total + xr[k].astype(F32)
    fin[...] = total.astype(BF16)
    arrival = exchange(
        [(fin, upd_o.at[x], device(x ^ k, y, z, c)) for k in range(1, n_leaf)], upd_o.at[pl.ds(0, n_leaf - 1)]
    )
    drains.append(fetch(fin, upd_o.at[x]))
    arrival.wait()
    for copy in drains:
        copy.wait()


def on_device(grid, n_leaf, right_side, panels, tile_counts, diag_leaf, diag_pair, diag_root, sup_rows):
    ny, nz, nc = grid
    levels, _, tiles, wide, _ = panels.shape
    rhs = right_side.shape[2]
    part, low = rhs // nc // nz, wide // ny
    rest = []
    for group in ROUNDS:
        size = len(group)
        bufs = [
            pltpu.VMEM((nc, size, rhs // nc, wide), BF16),
            pltpu.VMEM((size, rhs // nc, wide), BF16),
            pltpu.VMEM((nz, size, part, wide), BF16),
            pltpu.VMEM((nz - 1, size, part, wide), BF16),
            pltpu.VMEM((ny, size, part, low), BF16),
            pltpu.VMEM((ny - 1, size, part, low), BF16),
        ]
        for m in group:
            n = (1, 2, n_leaf, n_leaf)[m]
            bufs.append([pltpu.VMEM((part, low), F32), pltpu.VMEM((n * ny, part, low), F32)])
        rest.append(bufs)
    scratch = [
        pltpu.VMEM((tiles, rhs, wide), BF16),
        [pltpu.VMEM((tiles, wide, wide), BF16)] * levels,
        pltpu.VMEM((1, wide, wide), BF16),
        pltpu.VMEM((2, wide, wide), BF16),
        pltpu.VMEM((2, wide, wide), BF16),
        pltpu.VMEM((tiles, rhs, wide), F32),
        pltpu.VMEM((levels, rhs, wide), F32),
        pltpu.VMEM((levels, nc, nz, part, wide), BF16),
        pltpu.VMEM((tiles, rhs, wide), BF16),
        pltpu.VMEM((n_leaf - 1, rhs, wide), BF16),
        pltpu.VMEM((rhs, wide), BF16),
        rest,
        pltpu.SemaphoreType.DMA((SEMS,)),
    ]
    anywhere, scalars = pl.BlockSpec(memory_space=pl.ANY), pl.BlockSpec(memory_space=pltpu.SMEM)
    solved, updated = pl.pallas_call(
        functools.partial(kernel, grid, n_leaf),
        out_shape=(
            jax.ShapeDtypeStruct((levels, nc, nz, part, wide), BF16),
            jax.ShapeDtypeStruct((tiles, rhs, wide), BF16),
        ),
        in_specs=[scalars, scalars] + [anywhere] * 5,
        out_specs=(anywhere, anywhere),
        scratch_shapes=scratch,
        compiler_params=pltpu.CompilerParams(
            collective_id=0, has_side_effects=True, vmem_limit_bytes=56 * 2**20
        ),
    )(sup_rows, tile_counts, right_side, panels, diag_leaf, diag_pair, diag_root)
    return solved.reshape(levels, 1, rhs, wide), updated


def solution(mesh):
    placed = (
        P("leaf", "row", None, None),
        P(None, "leaf", "row", None, None),
        P(None, "leaf", "row"),
        P("leaf", None, None),
        P(),
        P(),
        P(),
    )
    return jax.shard_map(
        functools.partial(on_device, GRIDS[mesh.shape["row"]], mesh.shape["leaf"]),
        mesh=mesh,
        in_specs=placed,
        out_specs=(P(None, "leaf", None, None), P("row", None, None)),
        check_vma=False,
    )
```

time: 500 us -> 134 us (0.27)
  waiting for transfers between devices: 382 us -> 0 us
  Pallas kernels: 0 us -> 129 us
  blocking collectives: 39.5 us -> 0 us
  between operations: 24.4 us -> 0.64 us
  starting transfers between devices: 17.6 us -> 0 us
  matrix products: 11.5 us -> 0 us
  other arithmetic: 11.5 us -> 0 us
  local copies, waits for them, and re-layouts: 10.6 us -> 4.52 us
    all_gather x4 -> x0, waiting for transfers between devices: 344 us -> none  [picked(): lax.all_gather(shard, axis)]
    pallas_call x0 -> x1, Pallas kernels: none -> 129 us  [on_device(): pl.pallas_call(functools.partial(kernel, grid, n_leaf), out_shape=(jax.Sh...]
    psum x1 -> x0, blocking collectives: 39.5 us -> none  [on_device(): updated_side = lax.psum(share_parts - totals, 'leaf').astype(jnp.bfloat16)]
    all_to_all x4 -> x0, waiting for transfers between devices: 27 us -> none  [the longest x2 15.3 us: sum_at_owner(): lax.all_to_all(parts, axis, split_axis=0, concat_axis=0, tiled=True)]
    all_to_all x4 -> x0, starting transfers between devices: 16.2 us -> none  [the longest x2 8.24 us: sum_at_owner(): lax.all_to_all(parts, axis, split_axis=0, concat_axis=0, tiled=True)]
    dot_general x4 -> x0, matrix products: 11.5 us -> none  [on_device(): jnp.einsum('pi,bis->bps', current_solved, panels[panel_height, 0], prefer...]
    ppermute x1 -> x0, waiting for transfers between devices: 11.4 us -> none  [swapped(): lax.ppermute(shard, axis, [(i, i ^ 1 << apart) for i in range(lax.axis_si...]
    sub x3 -> x0, other arithmetic: 5.05 us -> none  [on_device(): lax.dynamic_index_in_dim(share_parts, local_tile, 0, keepdims=False)]
  transfers between devices with their start and end apart: 9 -> 0, of which waited for: 9 -> 0; matrix products, arithmetic and copies ran while one was open for 1% -> 0% of each run, Pallas kernels for 0% -> 0%
where the time goes in v1:
time: 134 us
  Pallas kernels  129 us (96%)
  local copies, waits for them, and re-layouts  4.52 us (3%)
    pallas_call x1, Pallas kernels, on_device(): pl.pallas_call(functools.partial(kernel, grid, n_leaf), out_shape=(jax.Sh...  129 us
    unnamed x2, local copies, waits for them, and re-layouts  4.52 us

profile of v1, /device:TPU:1, one launch (start us, length us, event | category | flops | bytes accessed | tf_op | source)
XLA Modules:
  0.0 133.9 jit_solution(2891623528396836809)
XLA Ops:
  0.6 128.7 %shard_map.86 = (bf16[4,2,8,16,512]{4,3,2,1,0:T(8,128)(2,1)}, bf16[4,256,512]{2,1,0:T(8,128)(2,1)}) custom-call(s32[4]{0:T(128)} %sup.1, s32[4,1,4]{2,1,0:T(1,128)} %cnt.1, bf16[1,4,256,512]{3,2,1,0:T(8,128)(2,1)} %rs_h.1, bf16[4,1,4,512,512]{4,3,2,1,0:T(8,128)(2,1)} %pan_h.1, bf16[1,512,512]{2,1,0:T(8,128)(2,1)} %dl_h.1, bf16[2,512,512]{2,1,0:T(8,128)(2,1)} %dp_h.1, ...), custom_call_target="tpu_custom_call" | custom-call | tf_op jit(solution)/shard_map/pallas_call | solution.py:230
  129.4 2.3 %copy.12 = bf16[4,1,256,512]{3,2,1,0:T(8,128)(2,1)} copy(bf16[4,1,256,512]{3,2,1,0:T(8,128)(2,1)} %bitcast.3) | data formatting | bytes 2097152
  131.6 2.3 %copy.13 = bf16[4,256,512]{2,1,0:T(8,128)(2,1)} copy(bf16[4,256,512]{2,1,0:T(8,128)(2,1)} %get-tuple-element.11) | data formatting | bytes 2097152

commit v2 on v1

v2 whole, which is shorter than its diff:
```python
import functools

import jax
import jax.numpy as jnp
from jax import lax
from jax.experimental import pallas as pl
from jax.experimental.pallas import tpu as pltpu
from jax.sharding import PartitionSpec as P

MESH = pl.DeviceIdType.MESH
F32, BF16 = jnp.float32, jnp.bfloat16
PAIRS = ((1, 2), (1, 3), (2, 3))
GRIDS = {64: (4, 8, 2), 8: (2, 2, 2)}
SEMS = 96


def meeting(level, n_leaf):
    return (1, 2, n_leaf, n_leaf)[level]


def kernel(grid, n_leaf, sup, cnt, rs_h, pan_h, dl_h, dp_h, dr_h, sol_o, upd_o, *scratch):
    ny, nz, nc = grid
    (rs, pan, dl, dp, dr, held, qacc, sol, base, xr, fin, slices, floods, pub, sem) = scratch
    levels, (tiles, wide, _) = len(pan), pan[0].shape
    rhs = rs.shape[1]
    low, mid, part = wide // ny, rhs // nc, rhs // nc // nz
    x, r = lax.axis_index("leaf"), lax.axis_index("row")
    y, z, c = r // (nz * nc), (r // nc) % nz, r % nc
    used = [0]
    drains = []

    def device(x_, y_, z_, c_):
        return (x_, (y_ * nz + z_) * nc + c_)

    def fresh():
        used[0] += 1
        assert used[0] <= SEMS
        return sem.at[used[0] - 1]

    def fetch(src, dst):
        copy = pltpu.make_async_copy(src, dst, fresh())
        copy.start()
        return copy

    def exchange(copies, whole):
        out, got = fresh(), fresh()
        for src, dst, dev in copies:
            pltpu.make_async_remote_copy(
                src_ref=src, dst_ref=dst, send_sem=out, recv_sem=got, device_id=dev, device_id_type=MESH
            ).start()
        drains.append(pltpu.make_async_copy(whole, whole, out))
        return pltpu.make_async_copy(whole, whole, got)

    def to_core(src, dst):
        return exchange([(src, dst, device(x, y, z, 1 - c))], dst)

    def scatter_z(src, dst):
        return exchange([(src.at[(z + k) % nz], dst.at[k - 1], device(x, y, (z + k) % nz, c)) for k in range(1, nz)], dst)

    def scatter_y(src, dst):
        return exchange([(src.at[(y + k) % ny], dst.at[k - 1], device(x, (y + k) % ny, z, c)) for k in range(1, ny)], dst)

    def gather_z(ref):
        return exchange(
            [(ref.at[z], ref.at[z], device(x, y, (z + k) % nz, c)) for k in range(1, nz)], ref.at[pl.ds(0, nz - 1)]
        )

    def total(mine, others):
        value = mine.astype(F32)
        for k in range(others.shape[0]):
            value = value + others[k].astype(F32)
        return value

    ready = {"rs": fetch(rs_h.at[0], rs), "d0": fetch(dl_h, dl)}
    for level, name in ((1, "p1"), (2, "p2"), (0, "p0"), (3, "p3")):
        ready[name] = fetch(pan_h.at[level, 0], pan[level])
    ready["d1"] = fetch(dp_h, dp)
    ready["d2"] = fetch(dr_h, dr)
    waited = set()

    def need(name):
        if name not in waited:
            waited.add(name)
            ready[name].wait()

    barrier = pltpu.get_barrier_semaphore()
    peers = [device(x, y, z, 1 - c)]
    peers += [device(x, y, (z + k) % nz, c) for k in range(1, nz)]
    peers += [device(x ^ i, (y + j) % ny, z, c) for i in range(n_leaf) for j in range(ny) if i or j]
    for dev in peers:
        pl.semaphore_signal(barrier, inc=1, device_id=dev, device_id_type=MESH)
    pl.semaphore_wait(barrier, len(peers))

    owner = [jnp.where(lax.div(sup[m], tiles) == r, 1.0, 0.0).astype(F32) for m in range(levels)]
    local = [lax.rem(sup[m], tiles) for m in range(levels)]
    columns = lax.broadcasted_iota(jnp.int32, (1, wide), 1)

    def product(level, tile, count):
        done = sol[level].reshape(rhs, wide)
        term = jnp.dot(done, pan[level][tile], preferred_element_type=F32)
        return jnp.where(columns < count, term, 0.0)

    def bulk(level):
        need(f"p{level}")

        def one(tile, carry):
            count = cnt[level, 0, tile]
            for m in range(level + 1):
                count = jnp.where(sup[m] == r * tiles + tile, 0, count)
            term = product(level, tile, count)
            before = rs[tile].astype(F32) if level == 0 else held[tile]
            held[tile] = before - term
            return carry

        lax.fori_loop(0, tiles, one, 0)

    def begin(m):
        qs, qr = slices[m][:2]
        rows = rs[local[m]].astype(F32)
        if m:
            rows = rows - qacc[m]
        rows = (rows * owner[m]).astype(BF16)
        for half in range(nc):
            qs[half] = rows[half * mid : (half + 1) * mid]
        return to_core(qs.at[1 - c], qr)

    def slice_z(m, arrival):
        qs, qr, zs, zr = slices[m][:4]
        arrival.wait()
        both = qs[c].astype(F32) + qr[...].astype(F32)
        zs[...] = both.astype(BF16).reshape(nz, part, wide)
        return scatter_z(zs, zr)

    def rows_of(m, arrival):
        zs, zr = slices[m][2:4]
        arrival.wait()
        return total(zs[z], zr).astype(BF16)

    def flood(m, value):
        n = meeting(m, n_leaf)
        cs, cr = floods[m]
        own = (x % n) * ny + y
        cs[...] = value
        cr[own] = value
        return exchange(
            [(cs, cr.at[own], device(x ^ a, (y + b) % ny, z, c)) for a in range(n) for b in range(ny) if a or b],
            cr.at[pl.ds(0, n * ny - 1)],
        )

    def solve(m, arrival):
        n = meeting(m, n_leaf)
        cr = floods[m][1]
        arrival.wait()
        if m < 2:
            merged = cr[0].astype(F32)
            for k in range(1, n * ny):
                merged = merged + cr[k].astype(F32)
            merged = merged.astype(BF16)
        else:
            parts = []
            for k in range(ny):
                value = cr[k]
                for a in range(1, n):
                    value = value + cr[a * ny + k]
                parts.append(value.astype(BF16))
            merged = jnp.concatenate(parts, axis=1)
        need(("d0", "d1", "d2", "d2")[m])
        inverse = dl[0] if m == 0 else dp[x // 2] if m == 1 else dr[m - 2]
        solved = jnp.dot(merged, inverse, preferred_element_type=F32).astype(BF16)
        sol[m, c, z] = solved
        return solved, gather_z(sol.at[m, c])

    def share(m, arrival):
        arrival.wait()
        return to_core(sol.at[m, c], sol.at[m, c])

    def keep(m, arrival):
        arrival.wait()
        drains.append(fetch(sol.at[m], sol_o.at[m]))

    pc, pcr, py, pyr, pz, pzr, pf = pub

    def publish_core():
        for i, (level, m) in enumerate(PAIRS):
            need(f"p{level}")
            live = jnp.where(columns < cnt[level, 0, local[m]], owner[m], 0.0).astype(BF16)
            tile = pan[level][local[m]] * live
            for half in range(nc):
                pc[half, i] = tile[half * (wide // nc) : (half + 1) * (wide // nc)]
        return to_core(pc.at[1 - c], pcr)

    def publish_columns(arrival):
        arrival.wait()
        for i in range(len(PAIRS)):
            both = (pc[c, i].astype(F32) + pcr[i].astype(F32)).astype(BF16)
            for k in range(ny):
                py[k, i] = both[:, k * low : (k + 1) * low]

    def publish_z(arrival):
        arrival.wait()
        step = wide // nc // nz
        for i in range(len(PAIRS)):
            value = py[y, i].astype(F32)
            for k in range(ny - 1):
                value = value + pyr[k, i].astype(F32)
            value = value.astype(BF16)
            for k in range(nz):
                pz[k, i] = value[k * step : (k + 1) * step]
        return scatter_z(pz, pzr)

    def publish_gather(arrival):
        arrival.wait()
        pf[c, z] = total(pz[z], pzr).astype(BF16)
        return gather_z(pf.at[c])

    def coupling(level, m):
        return pf[:, :, PAIRS.index((level, m))].reshape(wide, low)

    need("rs")
    arrival = slice_z(0, begin(0))
    publish_columns(publish_core())
    arrival = flood(0, rows_of(0, arrival))
    published = scatter_y(py, pyr)
    _, arrival = solve(0, arrival)
    published = publish_z(published)
    keep(0, share(0, arrival))
    need("p0")
    arrivals = {}
    for m in (1, 2, 3):
        qacc[m] = product(0, local[m], cnt[0, 0, local[m]])
        arrivals[m] = begin(m)
    for m in (1, 2, 3):
        arrivals[m] = slice_z(m, arrivals[m])
    published = publish_gather(published)
    bulk(0)
    merge1 = flood(1, rows_of(1, arrivals[1]))
    for m in (2, 3):
        rows = rows_of(m, arrivals[m])
        ys, yr = slices[m][4:]
        for k in range(ny):
            ys[k] = rows[:, k * low : (k + 1) * low]
        arrivals[m] = scatter_y(ys, yr)
    published.wait()
    published = to_core(pf.at[c], pf.at[c])
    solved1, spread1 = solve(1, merge1)
    published.wait()
    arrivals[2].wait()
    piece = total(slices[2][4][y], slices[2][5])
    merge2 = flood(2, piece - jnp.dot(solved1, coupling(1, 2), preferred_element_type=F32))
    arrivals[3].wait()
    piece = total(slices[3][4][y], slices[3][5])
    piece = piece - jnp.dot(solved1, coupling(1, 3), preferred_element_type=F32)
    spread1 = share(1, spread1)
    solved2, spread2 = solve(2, merge2)
    merge3 = flood(3, piece - jnp.dot(solved2, coupling(2, 3), preferred_element_type=F32))
    keep(1, spread1)
    bulk(1)
    spread2 = share(2, spread2)
    _, spread3 = solve(3, merge3)
    keep(2, spread2)
    bulk(2)
    keep(3, share(3, spread3))
    bulk(3)
    for tile in range(tiles):
        base[tile] = held[tile].astype(BF16)
    exchange([(base.at[x ^ k], xr.at[k - 1], device(x ^ k, y, z, c)) for k in range(1, n_leaf)], xr).wait()
    fin[...] = total(held[x], xr).astype(BF16)
    arrival = exchange(
        [(fin, upd_o.at[x], device(x ^ k, y, z, c)) for k in range(1, n_leaf)], upd_o.at[pl.ds(0, n_leaf - 1)]
    )
    drains.append(fetch(fin, upd_o.at[x]))
    arrival.wait()
    for copy in drains:
        copy.wait()


def on_device(grid, n_leaf, right_side, panels, tile_counts, diag_leaf, diag_pair, diag_root, sup_rows):
    ny, nz, nc = grid
    levels, _, tiles, wide, _ = panels.shape
    rhs = right_side.shape[2]
    mid, part, low = rhs // nc, rhs // nc // nz, wide // ny
    pairs, step = len(PAIRS), wide // nc // nz
    slices, floods = [], []
    for m in range(levels):
        slices.append(
            [
                pltpu.VMEM((nc, mid, wide), BF16),
                pltpu.VMEM((mid, wide), BF16),
                pltpu.VMEM((nz, part, wide), BF16),
                pltpu.VMEM((nz - 1, part, wide), BF16),
            ]
        )
        if m > 1:
            slices[m] += [pltpu.VMEM((ny, part, low), BF16), pltpu.VMEM((ny - 1, part, low), BF16)]
        piece, kind = ((part, wide), BF16) if m < 2 else ((part, low), F32)
        floods.append([pltpu.VMEM(piece, kind), pltpu.VMEM((meeting(m, n_leaf) * ny, *piece), kind)])
    pub = [
        pltpu.VMEM((nc, pairs, wide // nc, wide), BF16),
        pltpu.VMEM((pairs, wide // nc, wide), BF16),
        pltpu.VMEM((ny, pairs, wide // nc, low), BF16),
        pltpu.VMEM((ny - 1, pairs, wide // nc, low), BF16),
        pltpu.VMEM((nz, pairs, step, low), BF16),
        pltpu.VMEM((nz - 1, pairs, step, low), BF16),
        pltpu.VMEM((nc, nz, pairs, step, low), BF16),
    ]
    scratch = [
        pltpu.VMEM((tiles, rhs, wide), BF16),
        [pltpu.VMEM((tiles, wide, wide), BF16)] * levels,
        pltpu.VMEM((1, wide, wide), BF16),
        pltpu.VMEM((2, wide, wide), BF16),
        pltpu.VMEM((2, wide, wide), BF16),
        pltpu.VMEM((tiles, rhs, wide), F32),
        pltpu.VMEM((levels, rhs, wide), F32),
        pltpu.VMEM((levels, nc, nz, part, wide), BF16),
        pltpu.VMEM((tiles, rhs, wide), BF16),
        pltpu.VMEM((n_leaf - 1, rhs, wide), BF16),
        pltpu.VMEM((rhs, wide), BF16),
        slices,
        floods,
        pub,
        pltpu.SemaphoreType.DMA((SEMS,)),
    ]
    anywhere, scalars = pl.BlockSpec(memory_space=pl.ANY), pl.BlockSpec(memory_space=pltpu.SMEM)
    solved, updated = pl.pallas_call(
        functools.partial(kernel, grid, n_leaf),
        out_shape=(
            jax.ShapeDtypeStruct((levels, nc, nz, part, wide), BF16),
            jax.ShapeDtypeStruct((tiles, rhs, wide), BF16),
        ),
        in_specs=[scalars, scalars] + [anywhere] * 5,
        out_specs=(anywhere, anywhere),
        scratch_shapes=scratch,
        compiler_params=pltpu.CompilerParams(
            collective_id=0, has_side_effects=True, vmem_limit_bytes=56 * 2**20
        ),
    )(sup_rows, tile_counts, right_side, panels, diag_leaf, diag_pair, diag_root)
    return solved.reshape(levels, 1, rhs, wide), updated


def solution(mesh):
    placed = (
        P("leaf", "row", None, None),
        P(None, "leaf", "row", None, None),
        P(None, "leaf", "row"),
        P("leaf", None, None),
        P(),
        P(),
        P(),
    )
    return jax.shard_map(
        functools.partial(on_device, GRIDS[mesh.shape["row"]], mesh.shape["leaf"]),
        mesh=mesh,
        in_specs=placed,
        out_specs=(P(None, "leaf", None, None), P("row", None, None)),
        check_vma=False,
    )
```

time: 134 us -> 106 us (0.79)
  Pallas kernels: 129 us -> 100 us
    pallas_call x1, Pallas kernels: 129 us -> 100 us  [on_device(): pl.pallas_call(functools.partial(kernel, grid, n_leaf), out_shape=(jax.Sh...]
where the time goes in v2:
time: 106 us; the launch traced here: 105 us
  Pallas kernels  100 us (94%)
  local copies, waits for them, and re-layouts  4.52 us (4%)
    pallas_call x1, Pallas kernels, on_device(): pl.pallas_call(functools.partial(kernel, grid, n_leaf), out_shape=(jax.Sh...  100 us
    unnamed x2, local copies, waits for them, and re-layouts  4.52 us

profile of v2, /device:TPU:1, one launch (start us, length us, event | category | flops | bytes accessed | tf_op | source)
XLA Modules:
  0.0 105.2 jit_solution(10541487659734593429)
XLA Ops:
  0.6 100.0 %shard_map.86 = (bf16[4,2,8,16,512]{4,3,2,1,0:T(8,128)(2,1)}, bf16[4,256,512]{2,1,0:T(8,128)(2,1)}) custom-call(s32[4]{0:T(128)} %sup.1, s32[4,1,4]{2,1,0:T(1,128)} %cnt.1, bf16[1,4,256,512]{3,2,1,0:T(8,128)(2,1)} %rs_h.1, bf16[4,1,4,512,512]{4,3,2,1,0:T(8,128)(2,1)} %pan_h.1, bf16[1,512,512]{2,1,0:T(8,128)(2,1)} %dl_h.1, bf16[2,512,512]{2,1,0:T(8,128)(2,1)} %dp_h.1, ...), custom_call_target="tpu_custom_call" | custom-call | tf_op jit(solution)/shard_map/pallas_call | solution.py:324
  100.7 2.3 %copy.12 = bf16[4,1,256,512]{3,2,1,0:T(8,128)(2,1)} copy(bf16[4,1,256,512]{3,2,1,0:T(8,128)(2,1)} %bitcast.3) | data formatting | bytes 2097152
  103.0 2.3 %copy.13 = bf16[4,256,512]{2,1,0:T(8,128)(2,1)} copy(bf16[4,256,512]{2,1,0:T(8,128)(2,1)} %get-tuple-element.11) | data formatting | bytes 2097152

commit v3 on v2

--- a/solution.py
+++ b/solution.py
@@ -11,7 +11,7 @@
 F32, BF16 = jnp.float32, jnp.bfloat16
 PAIRS = ((1, 2), (1, 3), (2, 3))
 GRIDS = {64: (4, 8, 2), 8: (2, 2, 2)}
-SEMS = 96
+SEMS = 128
 
 
 def meeting(level, n_leaf):
@@ -20,7 +20,7 @@
 
 def kernel(grid, n_leaf, sup, cnt, rs_h, pan_h, dl_h, dp_h, dr_h, sol_o, upd_o, *scratch):
     ny, nz, nc = grid
-    (rs, pan, dl, dp, dr, held, qacc, sol, base, xr, fin, slices, floods, pub, sem) = scratch
+    (rs, pan, dl, dp, dr, held, qacc, sol, live, sums, acc, upd, folds, slices, floods, pub, sem) = scratch
     levels, (tiles, wide, _) = len(pan), pan[0].shape
     rhs = rs.shape[1]
     low, mid, part = wide // ny, rhs // nc, rhs // nc // nz
@@ -72,7 +72,7 @@
         return value
 
     ready = {"rs": fetch(rs_h.at[0], rs), "d0": fetch(dl_h, dl)}
-    for level, name in ((1, "p1"), (2, "p2"), (0, "p0"), (3, "p3")):
+    for level, name in ((1, "p1"), (2, "p2"), (3, "p3"), (0, "p0")):
         ready[name] = fetch(pan_h.at[level, 0], pan[level])
     ready["d1"] = fetch(dp_h, dp)
     ready["d2"] = fetch(dr_h, dr)
@@ -216,24 +216,87 @@
     def coupling(level, m):
         return pf[:, :, PAIRS.index((level, m))].reshape(wide, low)
 
+    def after(k):
+        return (x + k) % n_leaf
+
+    def fold(src, bufs):
+        relay, near = bufs[:2]
+        half = relay.shape[1]
+        first, second = pl.ds(0, half), pl.ds(half, half)
+        up, down = device(after(1), y, z, c), device(after(n_leaf - 1), y, z, c)
+        far = after(2)
+        relayed = exchange([(src.at[far, first], relay.at[0], up), (src.at[far, second], relay.at[1], down)], relay)
+        direct = exchange(
+            [(src.at[after(1), second], near.at[1], up), (src.at[after(n_leaf - 1), first], near.at[0], down)], near
+        )
+        return relayed, direct
+
+    def fold_on(src, bufs, relayed):
+        relay, _, out, last = bufs
+        half = relay.shape[1]
+        up, down = device(after(1), y, z, c), device(after(n_leaf - 1), y, z, c)
+        relayed.wait()
+        out[0] = (src[after(1), :half].astype(F32) + relay[0].astype(F32)).astype(BF16)
+        out[1] = (src[after(n_leaf - 1), half:].astype(F32) + relay[1].astype(F32)).astype(BF16)
+        return exchange([(out.at[0], last.at[0], up), (out.at[1], last.at[1], down)], last)
+
+    def folded(mine, bufs, i):
+        _, near, _, last = bufs
+        half = near.shape[1]
+        return mine[i * half : (i + 1) * half].astype(F32) + near[i].astype(F32) + last[i].astype(F32)
+
+    def mask_tiles(level):
+        need(f"p{level}")
+        into = live[level - 2]
+
+        def one(tile, carry):
+            count = cnt[level, 0, tile]
+            for m in range(level + 1):
+                count = jnp.where(sup[m] == r * tiles + tile, 0, count)
+            into[tile] = pan[level][tile] * jnp.where(columns < count, 1.0, 0.0).astype(BF16)
+            return carry
+
+        lax.fori_loop(0, tiles, one, 0)
+
+    def sum_tiles(level, arrivals):
+        for arrival in arrivals:
+            arrival.wait()
+        half = wide // 2
+        for i in range(2):
+            sums[level - 2, i * half : (i + 1) * half] = folded(live[level - 2][x], folds[level - 2], i).astype(BF16)
+
+    def take(level):
+        acc[...] = acc[...] - jnp.dot(sol[level].reshape(rhs, wide), sums[level - 2], preferred_element_type=F32)
+
     need("rs")
     arrival = slice_z(0, begin(0))
-    publish_columns(publish_core())
+    published = publish_core()
+    mask_tiles(3)
+    relayed3, direct3 = fold(live[1], folds[1])
+    publish_columns(published)
     arrival = flood(0, rows_of(0, arrival))
     published = scatter_y(py, pyr)
+    mask_tiles(2)
     _, arrival = solve(0, arrival)
+    last3 = fold_on(live[1], folds[1], relayed3)
     published = publish_z(published)
-    keep(0, share(0, arrival))
+    relayed2, direct2 = fold(live[0], folds[0])
+    shared = share(0, arrival)
+    keep(0, shared)
     need("p0")
     arrivals = {}
-    for m in (1, 2, 3):
+    for m in (1, 2):
         qacc[m] = product(0, local[m], cnt[0, 0, local[m]])
         arrivals[m] = begin(m)
-    for m in (1, 2, 3):
+    arrivals[1] = slice_z(1, arrivals[1])
+    published = publish_gather(published)
+    qacc[3] = product(0, local[3], cnt[0, 0, local[3]])
+    arrivals[3] = begin(3)
+    for m in (2, 3):
         arrivals[m] = slice_z(m, arrivals[m])
-    published = publish_gather(published)
+    merge1 = flood(1, rows_of(1, arrivals[1]))
     bulk(0)
-    merge1 = flood(1, rows_of(1, arrivals[1]))
+    last2 = fold_on(live[0], folds[0], relayed2)
     for m in (2, 3):
         rows = rows_of(m, arrivals[m])
         ys, yr = slices[m][4:]
@@ -250,26 +313,45 @@
     arrivals[3].wait()
     piece = total(slices[3][4][y], slices[3][5])
     piece = piece - jnp.dot(solved1, coupling(1, 3), preferred_element_type=F32)
-    spread1 = share(1, spread1)
+    sum_tiles(3, (direct3, last3))
     solved2, spread2 = solve(2, merge2)
     merge3 = flood(3, piece - jnp.dot(solved2, coupling(2, 3), preferred_element_type=F32))
-    keep(1, spread1)
+    keep(1, share(1, spread1))
     bulk(1)
-    spread2 = share(2, spread2)
+    for tile in range(tiles):
+        upd[tile] = held[tile].astype(BF16)
+    relayed, direct = fold(upd, folds[2])
     _, spread3 = solve(3, merge3)
-    keep(2, spread2)
-    bulk(2)
-    keep(3, share(3, spread3))
-    bulk(3)
-    for tile in range(tiles):
-        base[tile] = held[tile].astype(BF16)
-    exchange([(base.at[x ^ k], xr.at[k - 1], device(x ^ k, y, z, c)) for k in range(1, n_leaf)], xr).wait()
-    fin[...] = total(held[x], xr).astype(BF16)
-    arrival = exchange(
-        [(fin, upd_o.at[x], device(x ^ k, y, z, c)) for k in range(1, n_leaf)], upd_o.at[pl.ds(0, n_leaf - 1)]
-    )
-    drains.append(fetch(fin, upd_o.at[x]))
-    arrival.wait()
+    shared = share(2, spread2)
+    sum_tiles(2, (direct2, last2))
+    keep(2, shared)
+    last = fold_on(upd, folds[2], relayed)
+    shared = share(3, spread3)
+    direct.wait()
+    last.wait()
+    half = rhs // 2
+    for i in range(2):
+        acc[i * half : (i + 1) * half] = folded(held[x], folds[2], i)
+    take(2)
+    keep(3, shared)
+    take(3)
+    fin, got = folds[3]
+    for i in range(2):
+        fin[i] = acc[i * half : (i + 1) * half].astype(BF16)
+    up, down = device(after(1), y, z, c), device(after(n_leaf - 1), y, z, c)
+    ahead = exchange([(fin.at[0], got.at[0, 0], up), (fin.at[1], got.at[1, 1], down)], fin)
+    behind = exchange([(fin.at[1], got.at[0, 1], up), (fin.at[0], got.at[1, 0], down)], fin)
+    for i in range(2):
+        drains.append(fetch(fin.at[i], upd_o.at[x, pl.ds(i * half, half)]))
+    ahead.wait()
+    passed = exchange([(got.at[0, 0], got.at[2, 0], up), (got.at[1, 1], got.at[2, 1], down)], fin)
+    behind.wait()
+    for k, origin in ((0, after(n_leaf - 1)), (1, after(1))):
+        for i in range(2):
+            drains.append(fetch(got.at[k, i], upd_o.at[origin, pl.ds(i * half, half)]))
+    passed.wait()
+    for i in range(2):
+        drains.append(fetch(got.at[2, i], upd_o.at[after(2), pl.ds(i * half, half)]))
     for copy in drains:
         copy.wait()
 
@@ -312,9 +394,12 @@
         pltpu.VMEM((tiles, rhs, wide), F32),
         pltpu.VMEM((levels, rhs, wide), F32),
         pltpu.VMEM((levels, nc, nz, part, wide), BF16),
+        [pltpu.VMEM((tiles, wide, wide), BF16)] * 2,
+        pltpu.VMEM((2, wide, wide), BF16),
+        pltpu.VMEM((rhs, wide), F32),
         pltpu.VMEM((tiles, rhs, wide), BF16),
-        pltpu.VMEM((n_leaf - 1, rhs, wide), BF16),
-        pltpu.VMEM((rhs, wide), BF16),
+        [[pltpu.VMEM((2, length // 2, wide), BF16)] * 4 for length in (wide, wide, rhs)]
+        + [[pltpu.VMEM((2, rhs // 2, wide), BF16), pltpu.VMEM((n_leaf - 1, 2, rhs // 2, wide), BF16)]],
         slices,
         floods,
         pub,

time: 106 us -> 89.5 us (0.84)
  Pallas kernels: 100 us -> 84.1 us
    pallas_call x1, Pallas kernels: 100 us -> 84.1 us  [on_device(): pl.pallas_call(functools.partial(kernel, grid, n_leaf), out_shape=(jax.Sh...]
where the time goes in v3:
time: 89.5 us; the launch traced here: 89.3 us
  Pallas kernels  84.1 us (94%)
  local copies, waits for them, and re-layouts  4.52 us (5%)
    pallas_call x1, Pallas kernels, on_device(): pl.pallas_call(functools.partial(kernel, grid, n_leaf), out_shape=(jax.Sh...  84.1 us
    unnamed x2, local copies, waits for them, and re-layouts  4.52 us

profile of v3, /device:TPU:1, one launch (start us, length us, event | category | flops | bytes accessed | tf_op | source)
XLA Modules:
  0.0 89.3 jit_solution(9728202516485319822)
XLA Ops:
  0.6 84.1 %shard_map.86 = (bf16[4,2,8,16,512]{4,3,2,1,0:T(8,128)(2,1)}, bf16[4,256,512]{2,1,0:T(8,128)(2,1)}) custom-call(s32[4]{0:T(128)} %sup.1, s32[4,1,4]{2,1,0:T(1,128)} %cnt.1, bf16[1,4,256,512]{3,2,1,0:T(8,128)(2,1)} %rs_h.1, bf16[4,1,4,512,512]{4,3,2,1,0:T(8,128)(2,1)} %pan_h.1, bf16[1,512,512]{2,1,0:T(8,128)(2,1)} %dl_h.1, bf16[2,512,512]{2,1,0:T(8,128)(2,1)} %dp_h.1, ...), custom_call_target="tpu_custom_call" | custom-call | tf_op jit(solution)/shard_map/pallas_call | solution.py:409
  84.8 2.3 %copy.12 = bf16[4,1,256,512]{3,2,1,0:T(8,128)(2,1)} copy(bf16[4,1,256,512]{3,2,1,0:T(8,128)(2,1)} %bitcast.3) | data formatting | bytes 2097152
  87.0 2.3 %copy.13 = bf16[4,256,512]{2,1,0:T(8,128)(2,1)} copy(bf16[4,256,512]{2,1,0:T(8,128)(2,1)} %get-tuple-element.11) | data formatting | bytes 2097152

commit v4 on v3

--- a/solution.py
+++ b/solution.py
@@ -9,7 +9,7 @@
 
 MESH = pl.DeviceIdType.MESH
 F32, BF16 = jnp.float32, jnp.bfloat16
-PAIRS = ((1, 2), (1, 3), (2, 3))
+BATCHES = (((1, 2),), ((1, 3), (2, 3)))
 GRIDS = {64: (4, 8, 2), 8: (2, 2, 2)}
 SEMS = 128
 
@@ -178,28 +178,30 @@
         arrival.wait()
         drains.append(fetch(sol.at[m], sol_o.at[m]))
 
-    pc, pcr, py, pyr, pz, pzr, pf = pub
-
-    def publish_core():
-        for i, (level, m) in enumerate(PAIRS):
+    def publish_core(batch):
+        pc, pcr = pub[batch][:2]
+        for i, (level, m) in enumerate(BATCHES[batch]):
             need(f"p{level}")
-            live = jnp.where(columns < cnt[level, 0, local[m]], owner[m], 0.0).astype(BF16)
-            tile = pan[level][local[m]] * live
+            alive = jnp.where(columns < cnt[level, 0, local[m]], owner[m], 0.0).astype(BF16)
+            tile = pan[level][local[m]] * alive
             for half in range(nc):
                 pc[half, i] = tile[half * (wide // nc) : (half + 1) * (wide // nc)]
         return to_core(pc.at[1 - c], pcr)
 
-    def publish_columns(arrival):
-        arrival.wait()
-        for i in range(len(PAIRS)):
+    def publish_y(batch, arrival):
+        pc, pcr, py, pyr = pub[batch][:4]
+        arrival.wait()
+        for i in range(len(BATCHES[batch])):
             both = (pc[c, i].astype(F32) + pcr[i].astype(F32)).astype(BF16)
             for k in range(ny):
                 py[k, i] = both[:, k * low : (k + 1) * low]
-
-    def publish_z(arrival):
+        return scatter_y(py, pyr)
+
+    def publish_z(batch, arrival):
+        py, pyr, pz, pzr = pub[batch][2:6]
         arrival.wait()
         step = wide // nc // nz
-        for i in range(len(PAIRS)):
+        for i in range(len(BATCHES[batch])):
             value = py[y, i].astype(F32)
             for k in range(ny - 1):
                 value = value + pyr[k, i].astype(F32)
@@ -208,13 +210,20 @@
                 pz[k, i] = value[k * step : (k + 1) * step]
         return scatter_z(pz, pzr)
 
-    def publish_gather(arrival):
+    def publish_gather(batch, arrival):
+        pz, pzr, pf = pub[batch][4:]
         arrival.wait()
         pf[c, z] = total(pz[z], pzr).astype(BF16)
         return gather_z(pf.at[c])
 
+    def publish_last(batch, arrival):
+        pf = pub[batch][6]
+        arrival.wait()
+        return to_core(pf.at[c], pf.at[c])
+
     def coupling(level, m):
-        return pf[:, :, PAIRS.index((level, m))].reshape(wide, low)
+        batch = 0 if (level, m) in BATCHES[0] else 1
+        return pub[batch][6][:, :, BATCHES[batch].index((level, m))].reshape(wide, low)
 
     def after(k):
         return (x + k) % n_leaf
@@ -265,37 +274,40 @@
         for i in range(2):
             sums[level - 2, i * half : (i + 1) * half] = folded(live[level - 2][x], folds[level - 2], i).astype(BF16)
 
-    def take(level):
-        acc[...] = acc[...] - jnp.dot(sol[level].reshape(rhs, wide), sums[level - 2], preferred_element_type=F32)
+    def take(level, half):
+        done = sol[level, half].reshape(mid, wide)
+        return acc[half] - jnp.dot(done, sums[level - 2], preferred_element_type=F32)
 
     need("rs")
     arrival = slice_z(0, begin(0))
-    published = publish_core()
+    pub_a = publish_core(0)
+    pub_b = publish_core(1)
     mask_tiles(3)
     relayed3, direct3 = fold(live[1], folds[1])
-    publish_columns(published)
     arrival = flood(0, rows_of(0, arrival))
-    published = scatter_y(py, pyr)
+    pub_a = publish_y(0, pub_a)
+    pub_b = publish_y(1, pub_b)
     mask_tiles(2)
     _, arrival = solve(0, arrival)
+    pub_a = publish_z(0, pub_a)
     last3 = fold_on(live[1], folds[1], relayed3)
-    published = publish_z(published)
     relayed2, direct2 = fold(live[0], folds[0])
-    shared = share(0, arrival)
-    keep(0, shared)
+    keep(0, share(0, arrival))
     need("p0")
     arrivals = {}
     for m in (1, 2):
         qacc[m] = product(0, local[m], cnt[0, 0, local[m]])
         arrivals[m] = begin(m)
+    pub_a = publish_gather(0, pub_a)
     arrivals[1] = slice_z(1, arrivals[1])
-    published = publish_gather(published)
+    pub_b = publish_z(1, pub_b)
     qacc[3] = product(0, local[3], cnt[0, 0, local[3]])
     arrivals[3] = begin(3)
     for m in (2, 3):
         arrivals[m] = slice_z(m, arrivals[m])
+    pub_a = publish_last(0, pub_a)
     merge1 = flood(1, rows_of(1, arrivals[1]))
-    bulk(0)
+    pub_b = publish_gather(1, pub_b)
     last2 = fold_on(live[0], folds[0], relayed2)
     for m in (2, 3):
         rows = rows_of(m, arrivals[m])
@@ -303,17 +315,18 @@
         for k in range(ny):
             ys[k] = rows[:, k * low : (k + 1) * low]
         arrivals[m] = scatter_y(ys, yr)
-    published.wait()
-    published = to_core(pf.at[c], pf.at[c])
     solved1, spread1 = solve(1, merge1)
-    published.wait()
+    pub_a.wait()
     arrivals[2].wait()
     piece = total(slices[2][4][y], slices[2][5])
     merge2 = flood(2, piece - jnp.dot(solved1, coupling(1, 2), preferred_element_type=F32))
+    bulk(0)
+    pub_b = publish_last(1, pub_b)
+    sum_tiles(3, (direct3, last3))
     arrivals[3].wait()
     piece = total(slices[3][4][y], slices[3][5])
+    pub_b.wait()
     piece = piece - jnp.dot(solved1, coupling(1, 3), preferred_element_type=F32)
-    sum_tiles(3, (direct3, last3))
     solved2, spread2 = solve(2, merge2)
     merge3 = flood(3, piece - jnp.dot(solved2, coupling(2, 3), preferred_element_type=F32))
     keep(1, share(1, spread1))
@@ -324,36 +337,57 @@
     _, spread3 = solve(3, merge3)
     shared = share(2, spread2)
     sum_tiles(2, (direct2, last2))
+    last = fold_on(upd, folds[2], relayed)
     keep(2, shared)
-    last = fold_on(upd, folds[2], relayed)
-    shared = share(3, spread3)
     direct.wait()
     last.wait()
     half = rhs // 2
     for i in range(2):
-        acc[i * half : (i + 1) * half] = folded(held[x], folds[2], i)
-    take(2)
-    keep(3, shared)
-    take(3)
+        acc[i] = folded(held[x], folds[2], i)
+    for i in range(2):
+        acc[i] = take(2, i)
     fin, got = folds[3]
-    for i in range(2):
-        fin[i] = acc[i * half : (i + 1) * half].astype(BF16)
     up, down = device(after(1), y, z, c), device(after(n_leaf - 1), y, z, c)
-    ahead = exchange([(fin.at[0], got.at[0, 0], up), (fin.at[1], got.at[1, 1], down)], fin)
-    behind = exchange([(fin.at[1], got.at[0, 1], up), (fin.at[0], got.at[1, 0], down)], fin)
-    for i in range(2):
-        drains.append(fetch(fin.at[i], upd_o.at[x, pl.ds(i * half, half)]))
-    ahead.wait()
-    passed = exchange([(got.at[0, 0], got.at[2, 0], up), (got.at[1, 1], got.at[2, 1], down)], fin)
-    behind.wait()
+    shared = share(3, spread3)
+    sent = []
+    for i in (c, 1 - c):
+        fin[i] = take(3, i).astype(BF16)
+        sent.append(exchange([(fin.at[i], got.at[0, i], up), (fin.at[i], got.at[1, i], down)], got.at[0]))
+        drains.append(fetch(fin.at[i], upd_o.at[x, pl.ds(pl.multiple_of(i * half, half), half)]))
+        if len(sent) == 1:
+            keep(3, shared)
+    passed = []
+    for i, k, there in ((c, 0, up), (1 - c, 1, down)):
+        sent[k].wait()
+        passed.append(exchange([(got.at[k, i], got.at[2, i], there)], got.at[2, i]))
     for k, origin in ((0, after(n_leaf - 1)), (1, after(1))):
         for i in range(2):
             drains.append(fetch(got.at[k, i], upd_o.at[origin, pl.ds(i * half, half)]))
-    passed.wait()
-    for i in range(2):
-        drains.append(fetch(got.at[2, i], upd_o.at[after(2), pl.ds(i * half, half)]))
+    for i, arrival in zip((c, 1 - c), passed):
+        arrival.wait()
+        drains.append(fetch(got.at[2, i], upd_o.at[after(2), pl.ds(pl.multiple_of(i * half, half), half)]))
     for copy in drains:
         copy.wait()
+
+
+def settle(solved_h, updated_h, solved_o, updated_o, a, b, sem):
+    ways = []
+    for i, (src, mid, dst) in enumerate(((solved_h, a, solved_o), (updated_h, b, updated_o))):
+        for k in range(src.shape[0]):
+            spot = 2 * (i * src.shape[0] + k)
+            ways.append(
+                (
+                    pltpu.make_async_copy(src.at[k], mid.at[k], sem.at[spot]),
+                    pltpu.make_async_copy(mid.at[k], dst.at[k], sem.at[spot + 1]),
+                )
+            )
+    for into, _ in ways:
+        into.start()
+    for into, out in ways:
+        into.wait()
+        out.start()
+    for _, out in ways:
+        out.wait()
 
 
 def on_device(grid, n_leaf, right_side, panels, tile_counts, diag_leaf, diag_pair, diag_root, sup_rows):
@@ -361,7 +395,7 @@
     levels, _, tiles, wide, _ = panels.shape
     rhs = right_side.shape[2]
     mid, part, low = rhs // nc, rhs // nc // nz, wide // ny
-    pairs, step = len(PAIRS), wide // nc // nz
+    step = wide // nc // nz
     slices, floods = [], []
     for m in range(levels):
         slices.append(
@@ -377,13 +411,16 @@
         piece, kind = ((part, wide), BF16) if m < 2 else ((part, low), F32)
         floods.append([pltpu.VMEM(piece, kind), pltpu.VMEM((meeting(m, n_leaf) * ny, *piece), kind)])
     pub = [
-        pltpu.VMEM((nc, pairs, wide // nc, wide), BF16),
-        pltpu.VMEM((pairs, wide // nc, wide), BF16),
-        pltpu.VMEM((ny, pairs, wide // nc, low), BF16),
-        pltpu.VMEM((ny - 1, pairs, wide // nc, low), BF16),
-        pltpu.VMEM((nz, pairs, step, low), BF16),
-        pltpu.VMEM((nz - 1, pairs, step, low), BF16),
-        pltpu.VMEM((nc, nz, pairs, step, low), BF16),
+        [
+            pltpu.VMEM((nc, pairs, wide // nc, wide), BF16),
+            pltpu.VMEM((pairs, wide // nc, wide), BF16),
+            pltpu.VMEM((ny, pairs, wide // nc, low), BF16),
+            pltpu.VMEM((ny - 1, pairs, wide // nc, low), BF16),
+            pltpu.VMEM((nz, pairs, step, low), BF16),
+            pltpu.VMEM((nz - 1, pairs, step, low), BF16),
+            pltpu.VMEM((nc, nz, pairs, step, low), BF16),
+        ]
+        for pairs in map(len, BATCHES)
     ]
     scratch = [
         pltpu.VMEM((tiles, rhs, wide), BF16),
@@ -396,7 +433,7 @@
         pltpu.VMEM((levels, nc, nz, part, wide), BF16),
         [pltpu.VMEM((tiles, wide, wide), BF16)] * 2,
         pltpu.VMEM((2, wide, wide), BF16),
-        pltpu.VMEM((rhs, wide), F32),
+        pltpu.VMEM((2, mid, wide), F32),
         pltpu.VMEM((tiles, rhs, wide), BF16),
         [[pltpu.VMEM((2, length // 2, wide), BF16)] * 4 for length in (wide, wide, rhs)]
         + [[pltpu.VMEM((2, rhs // 2, wide), BF16), pltpu.VMEM((n_leaf - 1, 2, rhs // 2, wide), BF16)]],
@@ -419,6 +456,16 @@
             collective_id=0, has_side_effects=True, vmem_limit_bytes=56 * 2**20
         ),
     )(sup_rows, tile_counts, right_side, panels, diag_leaf, diag_pair, diag_root)
+    shapes = [solved.shape, updated.shape]
+    solved, updated = pl.pallas_call(
+        settle,
+        out_shape=tuple(jax.ShapeDtypeStruct(shape, BF16) for shape in shapes),
+        in_specs=[anywhere] * 2,
+        out_specs=(anywhere, anywhere),
+        scratch_shapes=[pltpu.VMEM(shape, BF16) for shape in shapes]
+        + [pltpu.SemaphoreType.DMA((2 * (levels + tiles),))],
+        compiler_params=pltpu.CompilerParams(vmem_limit_bytes=56 * 2**20),
+    )(solved, updated)
     return solved.reshape(levels, 1, rhs, wide), updated
 
 

time: 89.5 us -> 85.3 us (0.953)
  local copies, waits for them, and re-layouts: 4.52 us -> 0 us
    unnamed x2 -> x0, local copies, waits for them, and re-layouts: 4.52 us -> none
    pallas_call x0 -> x1, Pallas kernels: none -> 2.4 us  [on_device(): pl.pallas_call(settle, out_shape=tuple((jax.ShapeDtypeStruct(shape, BF16)...]
    pallas_call x1, Pallas kernels: 84.1 us -> 82.1 us  [on_device(): pl.pallas_call(functools.partial(kernel, grid, n_leaf), out_shape=(jax.Sh...]
where the time goes in v4:
time: 85.3 us; the launch traced here: 85.2 us
  Pallas kernels  84.5 us (99%)
    pallas_call x1, Pallas kernels, on_device(): pl.pallas_call(functools.partial(kernel, grid, n_leaf), out_shape=(jax.Sh...  82.1 us
    pallas_call x1, Pallas kernels, on_device(): pl.pallas_call(settle, out_shape=tuple((jax.ShapeDtypeStruct(shape, BF16)...  2.4 us

profile of v4, /device:TPU:1, one launch (start us, length us, event | category | flops | bytes accessed | tf_op | source)
XLA Modules:
  0.0 85.2 jit_solution(2327223236868399188)
XLA Ops:
  0.6 82.1 %shard_map.86 = (bf16[4,2,8,16,512]{4,3,2,1,0:T(8,128)(2,1)}, bf16[4,256,512]{2,1,0:T(8,128)(2,1)}) custom-call(s32[4]{0:T(128)} %sup.1, s32[4,1,4]{2,1,0:T(1,128)} %cnt.1, bf16[1,4,256,512]{3,2,1,0:T(8,128)(2,1)} %rs_h.1, bf16[4,1,4,512,512]{4,3,2,1,0:T(8,128)(2,1)} %pan_h.1, bf16[1,512,512]{2,1,0:T(8,128)(2,1)} %dl_h.1, bf16[2,512,512]{2,1,0:T(8,128)(2,1)} %dp_h.1, ...), custom_call_target="tpu_custom_call" | custom-call | tf_op jit(solution)/shard_map/pallas_call | solution.py:446
  82.8 2.4 %shard_map.87 = (bf16[4,2,8,16,512]{4,3,2,1,0:T(8,128)(2,1)}, bf16[4,256,512]{2,1,0:T(8,128)(2,1)}) custom-call(bf16[4,2,8,16,512]{4,3,2,1,0:T(8,128)(2,1)} %get-tuple-element.6.solved_h, bf16[4,256,512]{2,1,0:T(8,128)(2,1)} %get-tuple-element.7.updated_h), custom_call_target="tpu_custom_call" | custom-call | tf_op jit(solution)/shard_map/pallas_call | solution.py:460

commit v5 on v4

--- a/solution.py
+++ b/solution.py
@@ -71,6 +71,13 @@
             value = value + others[k].astype(F32)
         return value
 
+    barrier = pltpu.get_barrier_semaphore()
+    peers = [device(x, y, z, 1 - c)]
+    peers += [device(x, y, (z + k) % nz, c) for k in range(1, nz)]
+    peers += [device(x ^ i, (y + j) % ny, z, c) for i in range(n_leaf) for j in range(ny) if i or j]
+    for dev in peers:
+        pl.semaphore_signal(barrier, inc=1, device_id=dev, device_id_type=MESH)
+
     ready = {"rs": fetch(rs_h.at[0], rs), "d0": fetch(dl_h, dl)}
     for level, name in ((1, "p1"), (2, "p2"), (3, "p3"), (0, "p0")):
         ready[name] = fetch(pan_h.at[level, 0], pan[level])
@@ -83,14 +90,6 @@
             waited.add(name)
             ready[name].wait()
 
-    barrier = pltpu.get_barrier_semaphore()
-    peers = [device(x, y, z, 1 - c)]
-    peers += [device(x, y, (z + k) % nz, c) for k in range(1, nz)]
-    peers += [device(x ^ i, (y + j) % ny, z, c) for i in range(n_leaf) for j in range(ny) if i or j]
-    for dev in peers:
-        pl.semaphore_signal(barrier, inc=1, device_id=dev, device_id_type=MESH)
-    pl.semaphore_wait(barrier, len(peers))
-
     owner = [jnp.where(lax.div(sup[m], tiles) == r, 1.0, 0.0).astype(F32) for m in range(levels)]
     local = [lax.rem(sup[m], tiles) for m in range(levels)]
     columns = lax.broadcasted_iota(jnp.int32, (1, wide), 1)
@@ -100,29 +99,54 @@
         term = jnp.dot(done, pan[level][tile], preferred_element_type=F32)
         return jnp.where(columns < count, term, 0.0)
 
+    def update(level, tile):
+        count = cnt[level, 0, tile]
+        for m in range(level + 1):
+            count = jnp.where(sup[m] == r * tiles + tile, 0, count)
+        term = product(level, tile, count)
+        before = rs[tile].astype(F32) if level == 0 else held[tile]
+        held[tile] = before - term
+
     def bulk(level):
         need(f"p{level}")
 
         def one(tile, carry):
-            count = cnt[level, 0, tile]
-            for m in range(level + 1):
-                count = jnp.where(sup[m] == r * tiles + tile, 0, count)
-            term = product(level, tile, count)
-            before = rs[tile].astype(F32) if level == 0 else held[tile]
-            held[tile] = before - term
+            update(level, tile)
             return carry
 
         lax.fori_loop(0, tiles, one, 0)
 
-    def begin(m):
-        qs, qr = slices[m][:2]
+    def prepare(m):
+        qs = slices[m][0]
         rows = rs[local[m]].astype(F32)
         if m:
             rows = rows - qacc[m]
         rows = (rows * owner[m]).astype(BF16)
         for half in range(nc):
             qs[half] = rows[half * mid : (half + 1) * mid]
+
+    def begin(m):
+        qs, qr = slices[m][:2]
         return to_core(qs.at[1 - c], qr)
+
+    def columns_y(m, arrival):
+        qs, qr, ys, yr = slices[m][:4]
+        arrival.wait()
+        both = (qs[c].astype(F32) + qr[...].astype(F32)).astype(BF16)
+        for k in range(ny):
+            ys[k] = both[:, k * low : (k + 1) * low]
+        return scatter_y(ys, yr)
+
+    def rows_z(m, arrival):
+        ys, yr, zs, zr = slices[m][2:]
+        arrival.wait()
+        zs[...] = total(ys[y], yr).astype(BF16).reshape(nz, part, low)
+        return scatter_z(zs, zr)
+
+    def piece_of(m, arrival):
+        zs, zr = slices[m][4:]
+        arrival.wait()
+        return total(zs[z], zr)
 
     def slice_z(m, arrival):
         qs, qr, zs, zr = slices[m][:4]
@@ -178,14 +202,17 @@
         arrival.wait()
         drains.append(fetch(sol.at[m], sol_o.at[m]))
 
-    def publish_core(batch):
-        pc, pcr = pub[batch][:2]
+    def publish_prepare(batch):
+        pc = pub[batch][0]
         for i, (level, m) in enumerate(BATCHES[batch]):
             need(f"p{level}")
             alive = jnp.where(columns < cnt[level, 0, local[m]], owner[m], 0.0).astype(BF16)
             tile = pan[level][local[m]] * alive
             for half in range(nc):
                 pc[half, i] = tile[half * (wide // nc) : (half + 1) * (wide // nc)]
+
+    def publish_core(batch):
+        pc, pcr = pub[batch][:2]
         return to_core(pc.at[1 - c], pcr)
 
     def publish_y(batch, arrival):
@@ -228,26 +255,34 @@
     def after(k):
         return (x + k) % n_leaf
 
-    def fold(src, bufs):
-        relay, near = bufs[:2]
+    up, down = device(after(1), y, z, c), device(after(n_leaf - 1), y, z, c)
+
+    def fold_far(src, bufs):
+        relay = bufs[0]
         half = relay.shape[1]
-        first, second = pl.ds(0, half), pl.ds(half, half)
-        up, down = device(after(1), y, z, c), device(after(n_leaf - 1), y, z, c)
-        far = after(2)
-        relayed = exchange([(src.at[far, first], relay.at[0], up), (src.at[far, second], relay.at[1], down)], relay)
-        direct = exchange(
-            [(src.at[after(1), second], near.at[1], up), (src.at[after(n_leaf - 1), first], near.at[0], down)], near
+        far, first, second = after(2), pl.ds(0, half), pl.ds(half, half)
+        return exchange([(src.at[far, first], relay.at[0], up), (src.at[far, second], relay.at[1], down)], relay)
+
+    def fold_near(src, bufs, piece=0, pieces=1):
+        near = bufs[1]
+        half, size = near.shape[1], near.shape[1] // pieces
+        rows, first, second = pl.ds(piece * size, size), pl.ds(piece * size, size), pl.ds(half + piece * size, size)
+        return exchange(
+            [
+                (src.at[after(1), second], near.at[1, rows], up),
+                (src.at[after(n_leaf - 1), first], near.at[0, rows], down),
+            ],
+            near.at[:, rows],
         )
-        return relayed, direct
-
-    def fold_on(src, bufs, relayed):
+
+    def fold_on(src, bufs, piece=0, pieces=1):
         relay, _, out, last = bufs
-        half = relay.shape[1]
-        up, down = device(after(1), y, z, c), device(after(n_leaf - 1), y, z, c)
-        relayed.wait()
-        out[0] = (src[after(1), :half].astype(F32) + relay[0].astype(F32)).astype(BF16)
-        out[1] = (src[after(n_leaf - 1), half:].astype(F32) + relay[1].astype(F32)).astype(BF16)
-        return exchange([(out.at[0], last.at[0], up), (out.at[1], last.at[1], down)], last)
+        half, size = relay.shape[1], relay.shape[1] // pieces
+        a, b = piece * size, (piece + 1) * size
+        out[0, a:b] = (src[after(1), a:b].astype(F32) + relay[0, a:b].astype(F32)).astype(BF16)
+        out[1, a:b] = (src[after(n_leaf - 1), half + a : half + b].astype(F32) + relay[1, a:b].astype(F32)).astype(BF16)
+        rows = pl.ds(a, size)
+        return exchange([(out.at[0, rows], last.at[0, rows], up), (out.at[1, rows], last.at[1, rows], down)], last.at[:, rows])
 
     def folded(mine, bufs, i):
         _, near, _, last = bufs
@@ -279,65 +314,83 @@
         return acc[half] - jnp.dot(done, sums[level - 2], preferred_element_type=F32)
 
     need("rs")
-    arrival = slice_z(0, begin(0))
+    prepare(0)
+    pl.semaphore_wait(barrier, len(peers))
+    arrival = begin(0)
+    publish_prepare(0)
     pub_a = publish_core(0)
+    arrival = slice_z(0, arrival)
+    publish_prepare(1)
     pub_b = publish_core(1)
     mask_tiles(3)
-    relayed3, direct3 = fold(live[1], folds[1])
+    relayed3 = fold_far(live[1], folds[1])
+    direct3 = fold_near(live[1], folds[1])
     arrival = flood(0, rows_of(0, arrival))
     pub_a = publish_y(0, pub_a)
     pub_b = publish_y(1, pub_b)
     mask_tiles(2)
     _, arrival = solve(0, arrival)
     pub_a = publish_z(0, pub_a)
-    last3 = fold_on(live[1], folds[1], relayed3)
-    relayed2, direct2 = fold(live[0], folds[0])
+    relayed3.wait()
+    last3 = fold_on(live[1], folds[1])
+    relayed2 = fold_far(live[0], folds[0])
+    direct2 = [fold_near(live[0], folds[0], 0, 2)]
     keep(0, share(0, arrival))
     need("p0")
     arrivals = {}
-    for m in (1, 2):
+
+    def depart(m):
         qacc[m] = product(0, local[m], cnt[0, 0, local[m]])
+        prepare(m)
         arrivals[m] = begin(m)
+
+    depart(1)
+    depart(2)
+    arrivals[1] = slice_z(1, arrivals[1])
     pub_a = publish_gather(0, pub_a)
-    arrivals[1] = slice_z(1, arrivals[1])
+    arrivals[2] = columns_y(2, arrivals[2])
+    depart(3)
     pub_b = publish_z(1, pub_b)
-    qacc[3] = product(0, local[3], cnt[0, 0, local[3]])
-    arrivals[3] = begin(3)
+    arrivals[3] = columns_y(3, arrivals[3])
+    merge1 = flood(1, rows_of(1, arrivals[1]))
     for m in (2, 3):
-        arrivals[m] = slice_z(m, arrivals[m])
+        arrivals[m] = rows_z(m, arrivals[m])
+    direct2.append(fold_near(live[0], folds[0], 1, 2))
+    relayed2.wait()
+    last2 = [fold_on(live[0], folds[0], 0, 2)]
     pub_a = publish_last(0, pub_a)
-    merge1 = flood(1, rows_of(1, arrivals[1]))
     pub_b = publish_gather(1, pub_b)
-    last2 = fold_on(live[0], folds[0], relayed2)
-    for m in (2, 3):
-        rows = rows_of(m, arrivals[m])
-        ys, yr = slices[m][4:]
-        for k in range(ny):
-            ys[k] = rows[:, k * low : (k + 1) * low]
-        arrivals[m] = scatter_y(ys, yr)
     solved1, spread1 = solve(1, merge1)
     pub_a.wait()
-    arrivals[2].wait()
-    piece = total(slices[2][4][y], slices[2][5])
+    piece = piece_of(2, arrivals[2])
     merge2 = flood(2, piece - jnp.dot(solved1, coupling(1, 2), preferred_element_type=F32))
+    last2.append(fold_on(live[0], folds[0], 1, 2))
+    pub_b = publish_last(1, pub_b)
     bulk(0)
-    pub_b = publish_last(1, pub_b)
     sum_tiles(3, (direct3, last3))
-    arrivals[3].wait()
-    piece = total(slices[3][4][y], slices[3][5])
+    piece = piece_of(3, arrivals[3])
     pub_b.wait()
     piece = piece - jnp.dot(solved1, coupling(1, 3), preferred_element_type=F32)
     solved2, spread2 = solve(2, merge2)
     merge3 = flood(3, piece - jnp.dot(solved2, coupling(2, 3), preferred_element_type=F32))
     keep(1, share(1, spread1))
-    bulk(1)
-    for tile in range(tiles):
+    need("p1")
+
+    def settle_base(tile):
+        update(1, tile)
         upd[tile] = held[tile].astype(BF16)
-    relayed, direct = fold(upd, folds[2])
+
+    settle_base(after(2))
+    relayed = fold_far(upd, folds[2])
+    settle_base(after(1))
+    settle_base(after(n_leaf - 1))
+    direct = fold_near(upd, folds[2])
+    update(1, x)
     _, spread3 = solve(3, merge3)
+    relayed.wait()
+    last = fold_on(upd, folds[2])
     shared = share(2, spread2)
-    sum_tiles(2, (direct2, last2))
-    last = fold_on(upd, folds[2], relayed)
+    sum_tiles(2, direct2 + last2)
     keep(2, shared)
     direct.wait()
     last.wait()
@@ -347,7 +400,6 @@
     for i in range(2):
         acc[i] = take(2, i)
     fin, got = folds[3]
-    up, down = device(after(1), y, z, c), device(after(n_leaf - 1), y, z, c)
     shared = share(3, spread3)
     sent = []
     for i in (c, 1 - c):
@@ -398,16 +450,10 @@
     step = wide // nc // nz
     slices, floods = [], []
     for m in range(levels):
-        slices.append(
-            [
-                pltpu.VMEM((nc, mid, wide), BF16),
-                pltpu.VMEM((mid, wide), BF16),
-                pltpu.VMEM((nz, part, wide), BF16),
-                pltpu.VMEM((nz - 1, part, wide), BF16),
-            ]
-        )
-        if m > 1:
-            slices[m] += [pltpu.VMEM((ny, part, low), BF16), pltpu.VMEM((ny - 1, part, low), BF16)]
+        spread = [((nz, part), wide)] if m < 2 else [((ny, mid), low), ((nz, part), low)]
+        slices.append([pltpu.VMEM((nc, mid, wide), BF16), pltpu.VMEM((mid, wide), BF16)])
+        for (ways, rows), length in spread:
+            slices[m] += [pltpu.VMEM((ways, rows, length), BF16), pltpu.VMEM((ways - 1, rows, length), BF16)]
         piece, kind = ((part, wide), BF16) if m < 2 else ((part, low), F32)
         floods.append([pltpu.VMEM(piece, kind), pltpu.VMEM((meeting(m, n_leaf) * ny, *piece), kind)])
     pub = [

time: 85.3 us -> 82 us (0.961)
  Pallas kernels: 84.5 us -> 81 us
    pallas_call x1, Pallas kernels: 82.1 us -> 78.6 us  [on_device(): pl.pallas_call(functools.partial(kernel, grid, n_leaf), out_shape=(jax.Sh...]
where the time goes in v5:
time: 82 us; the launch traced here: 81.6 us
  Pallas kernels  81 us (99%)
    pallas_call x1, Pallas kernels, on_device(): pl.pallas_call(functools.partial(kernel, grid, n_leaf), out_shape=(jax.Sh...  78.6 us
    pallas_call x1, Pallas kernels, on_device(): pl.pallas_call(settle, out_shape=tuple((jax.ShapeDtypeStruct(shape, BF16)...  2.4 us

profile of v5, /device:TPU:1, one launch (start us, length us, event | category | flops | bytes accessed | tf_op | source)
XLA Modules:
  0.0 81.6 jit_solution(15207541202999230806)
XLA Ops:
  0.6 78.6 %shard_map.86 = (bf16[4,2,8,16,512]{4,3,2,1,0:T(8,128)(2,1)}, bf16[4,256,512]{2,1,0:T(8,128)(2,1)}) custom-call(s32[4]{0:T(128)} %sup.1, s32[4,1,4]{2,1,0:T(1,128)} %cnt.1, bf16[1,4,256,512]{3,2,1,0:T(8,128)(2,1)} %rs_h.1, bf16[4,1,4,512,512]{4,3,2,1,0:T(8,128)(2,1)} %pan_h.1, bf16[1,512,512]{2,1,0:T(8,128)(2,1)} %dl_h.1, bf16[2,512,512]{2,1,0:T(8,128)(2,1)} %dp_h.1, ...), custom_call_target="tpu_custom_call" | custom-call | tf_op jit(solution)/shard_map/pallas_call | solution.py:492
  79.2 2.4 %shard_map.87 = (bf16[4,2,8,16,512]{4,3,2,1,0:T(8,128)(2,1)}, bf16[4,256,512]{2,1,0:T(8,128)(2,1)}) custom-call(bf16[4,2,8,16,512]{4,3,2,1,0:T(8,128)(2,1)} %get-tuple-element.6.solved_h, bf16[4,256,512]{2,1,0:T(8,128)(2,1)} %get-tuple-element.7.updated_h), custom_call_target="tpu_custom_call" | custom-call | tf_op jit(solution)/shard_map/pallas_call | solution.py:506

commit v6 on v5

--- a/solution.py
+++ b/solution.py
@@ -20,7 +20,7 @@
 
 def kernel(grid, n_leaf, sup, cnt, rs_h, pan_h, dl_h, dp_h, dr_h, sol_o, upd_o, *scratch):
     ny, nz, nc = grid
-    (rs, pan, dl, dp, dr, held, qacc, sol, live, sums, acc, upd, folds, slices, floods, pub, sem) = scratch
+    (rs, pan, dl, dp, dr, held, first, sol, live, sums, acc, upd, folds, slices, floods, pub, sem) = scratch
     levels, (tiles, wide, _) = len(pan), pan[0].shape
     rhs = rs.shape[1]
     low, mid, part = wide // ny, rhs // nc, rhs // nc // nz
@@ -71,14 +71,15 @@
             value = value + others[k].astype(F32)
         return value
 
+    ready = {"rs": fetch(rs_h.at[0], rs)}
     barrier = pltpu.get_barrier_semaphore()
-    peers = [device(x, y, z, 1 - c)]
-    peers += [device(x, y, (z + k) % nz, c) for k in range(1, nz)]
+    peers = [device(x, y, (z + k) % nz, c) for k in sorted(range(1, nz), key=lambda k: abs(k - nz // 2))]
     peers += [device(x ^ i, (y + j) % ny, z, c) for i in range(n_leaf) for j in range(ny) if i or j]
+    peers += [device(x, y, z, 1 - c)]
     for dev in peers:
         pl.semaphore_signal(barrier, inc=1, device_id=dev, device_id_type=MESH)
 
-    ready = {"rs": fetch(rs_h.at[0], rs), "d0": fetch(dl_h, dl)}
+    ready["d0"] = fetch(dl_h, dl)
     for level, name in ((1, "p1"), (2, "p2"), (3, "p3"), (0, "p0")):
         ready[name] = fetch(pan_h.at[level, 0], pan[level])
     ready["d1"] = fetch(dp_h, dp)
@@ -118,10 +119,7 @@
 
     def prepare(m):
         qs = slices[m][0]
-        rows = rs[local[m]].astype(F32)
-        if m:
-            rows = rows - qacc[m]
-        rows = (rows * owner[m]).astype(BF16)
+        rows = rs[local[m]] * owner[m].astype(BF16)
         for half in range(nc):
             qs[half] = rows[half * mid : (half + 1) * mid]
 
@@ -130,9 +128,8 @@
         return to_core(qs.at[1 - c], qr)
 
     def columns_y(m, arrival):
-        qs, qr, ys, yr = slices[m][:4]
-        arrival.wait()
-        both = (qs[c].astype(F32) + qr[...].astype(F32)).astype(BF16)
+        ys, yr = slices[m][2:4]
+        both = half_of(m, arrival)
         for k in range(ny):
             ys[k] = both[:, k * low : (k + 1) * low]
         return scatter_y(ys, yr)
@@ -148,11 +145,17 @@
         arrival.wait()
         return total(zs[z], zr)
 
+    def half_of(m, arrival):
+        qs, qr = slices[m][:2]
+        arrival.wait()
+        both = qs[c].astype(F32) + qr[...].astype(F32)
+        if m:
+            both = both - jnp.dot(sol[0, c].reshape(mid, wide), first[1][m - 1], preferred_element_type=F32)
+        return both.astype(BF16)
+
     def slice_z(m, arrival):
-        qs, qr, zs, zr = slices[m][:4]
-        arrival.wait()
-        both = qs[c].astype(F32) + qr[...].astype(F32)
-        zs[...] = both.astype(BF16).reshape(nz, part, wide)
+        zs, zr = slices[m][2:4]
+        zs[...] = half_of(m, arrival).reshape(nz, part, wide)
         return scatter_z(zs, zr)
 
     def rows_of(m, arrival):
@@ -202,6 +205,13 @@
         arrival.wait()
         drains.append(fetch(sol.at[m], sol_o.at[m]))
 
+    def first_core():
+        need("p0")
+        for m in range(1, levels):
+            alive = jnp.where(columns < cnt[0, 0, local[m]], owner[m], 0.0).astype(BF16)
+            first[0][m - 1] = pan[0][local[m]] * alive
+        return to_core(first[0], first[1])
+
     def publish_prepare(batch):
         pc = pub[batch][0]
         for i, (level, m) in enumerate(BATCHES[batch]):
@@ -257,22 +267,21 @@
 
     up, down = device(after(1), y, z, c), device(after(n_leaf - 1), y, z, c)
 
-    def fold_far(src, bufs):
+    def fold_far(src, bufs, piece=0, pieces=1):
         relay = bufs[0]
-        half = relay.shape[1]
-        far, first, second = after(2), pl.ds(0, half), pl.ds(half, half)
-        return exchange([(src.at[far, first], relay.at[0], up), (src.at[far, second], relay.at[1], down)], relay)
-
-    def fold_near(src, bufs, piece=0, pieces=1):
+        half, size = relay.shape[1], relay.shape[1] // pieces
+        far, rows, second = after(2), pl.ds(piece * size, size), pl.ds(half + piece * size, size)
+        return exchange(
+            [(src.at[far, rows], relay.at[0, rows], up), (src.at[far, second], relay.at[1, rows], down)],
+            relay.at[:, rows],
+        )
+
+    def fold_near(src, bufs):
         near = bufs[1]
-        half, size = near.shape[1], near.shape[1] // pieces
-        rows, first, second = pl.ds(piece * size, size), pl.ds(piece * size, size), pl.ds(half + piece * size, size)
+        half = near.shape[1]
+        first, second = pl.ds(0, half), pl.ds(half, half)
         return exchange(
-            [
-                (src.at[after(1), second], near.at[1, rows], up),
-                (src.at[after(n_leaf - 1), first], near.at[0, rows], down),
-            ],
-            near.at[:, rows],
+            [(src.at[after(1), second], near.at[1], up), (src.at[after(n_leaf - 1), first], near.at[0], down)], near
         )
 
     def fold_on(src, bufs, piece=0, pieces=1):
@@ -319,61 +328,58 @@
     arrival = begin(0)
     publish_prepare(0)
     pub_a = publish_core(0)
+    mask_tiles(3)
+    relayed3 = fold_far(live[1], folds[1])
+    direct3 = fold_near(live[1], folds[1])
     arrival = slice_z(0, arrival)
     publish_prepare(1)
     pub_b = publish_core(1)
-    mask_tiles(3)
-    relayed3 = fold_far(live[1], folds[1])
-    direct3 = fold_near(live[1], folds[1])
+    arrivals = {}
+    for m in (1, 2, 3):
+        prepare(m)
+        arrivals[m] = begin(m)
+    coupled = first_core()
     arrival = flood(0, rows_of(0, arrival))
     pub_a = publish_y(0, pub_a)
     pub_b = publish_y(1, pub_b)
     mask_tiles(2)
-    _, arrival = solve(0, arrival)
-    pub_a = publish_z(0, pub_a)
     relayed3.wait()
     last3 = fold_on(live[1], folds[1])
     relayed2 = fold_far(live[0], folds[0])
-    direct2 = [fold_near(live[0], folds[0], 0, 2)]
-    keep(0, share(0, arrival))
-    need("p0")
-    arrivals = {}
-
-    def depart(m):
-        qacc[m] = product(0, local[m], cnt[0, 0, local[m]])
-        prepare(m)
-        arrivals[m] = begin(m)
-
-    depart(1)
-    depart(2)
+    _, arrival = solve(0, arrival)
+    coupled.wait()
+    for m in range(1, levels):
+        first[1][m - 1] = first[0][m - 1] + first[1][m - 1]
+    pub_a = publish_z(0, pub_a)
+    shared0 = share(0, arrival)
     arrivals[1] = slice_z(1, arrivals[1])
     pub_a = publish_gather(0, pub_a)
     arrivals[2] = columns_y(2, arrivals[2])
-    depart(3)
     pub_b = publish_z(1, pub_b)
     arrivals[3] = columns_y(3, arrivals[3])
     merge1 = flood(1, rows_of(1, arrivals[1]))
     for m in (2, 3):
         arrivals[m] = rows_z(m, arrivals[m])
-    direct2.append(fold_near(live[0], folds[0], 1, 2))
-    relayed2.wait()
-    last2 = [fold_on(live[0], folds[0], 0, 2)]
+    direct2 = fold_near(live[0], folds[0])
     pub_a = publish_last(0, pub_a)
     pub_b = publish_gather(1, pub_b)
     solved1, spread1 = solve(1, merge1)
     pub_a.wait()
     piece = piece_of(2, arrivals[2])
     merge2 = flood(2, piece - jnp.dot(solved1, coupling(1, 2), preferred_element_type=F32))
-    last2.append(fold_on(live[0], folds[0], 1, 2))
+    relayed2.wait()
+    last2 = fold_on(live[0], folds[0])
     pub_b = publish_last(1, pub_b)
+    keep(0, shared0)
     bulk(0)
     sum_tiles(3, (direct3, last3))
     piece = piece_of(3, arrivals[3])
     pub_b.wait()
     piece = piece - jnp.dot(solved1, coupling(1, 3), preferred_element_type=F32)
+    shared1 = share(1, spread1)
     solved2, spread2 = solve(2, merge2)
     merge3 = flood(3, piece - jnp.dot(solved2, coupling(2, 3), preferred_element_type=F32))
-    keep(1, share(1, spread1))
+    keep(1, shared1)
     need("p1")
 
     def settle_base(tile):
@@ -381,19 +387,21 @@
         upd[tile] = held[tile].astype(BF16)
 
     settle_base(after(2))
-    relayed = fold_far(upd, folds[2])
+    relayed = [fold_far(upd, folds[2], i, 2) for i in range(2)]
     settle_base(after(1))
     settle_base(after(n_leaf - 1))
     direct = fold_near(upd, folds[2])
     update(1, x)
     _, spread3 = solve(3, merge3)
-    relayed.wait()
-    last = fold_on(upd, folds[2])
+    last = []
+    for i in range(2):
+        relayed[i].wait()
+        last.append(fold_on(upd, folds[2], i, 2))
     shared = share(2, spread2)
-    sum_tiles(2, direct2 + last2)
+    sum_tiles(2, (direct2, last2))
     keep(2, shared)
-    direct.wait()
-    last.wait()
+    for arrival in (direct, *last):
+        arrival.wait()
     half = rhs // 2
     for i in range(2):
         acc[i] = folded(held[x], folds[2], i)
@@ -401,23 +409,36 @@
         acc[i] = take(2, i)
     fin, got = folds[3]
     shared = share(3, spread3)
-    sent = []
-    for i in (c, 1 - c):
-        fin[i] = take(3, i).astype(BF16)
-        sent.append(exchange([(fin.at[i], got.at[0, i], up), (fin.at[i], got.at[1, i], down)], got.at[0]))
-        drains.append(fetch(fin.at[i], upd_o.at[x, pl.ds(pl.multiple_of(i * half, half), half)]))
-        if len(sent) == 1:
-            keep(3, shared)
-    passed = []
-    for i, k, there in ((c, 0, up), (1 - c, 1, down)):
-        sent[k].wait()
-        passed.append(exchange([(got.at[k, i], got.at[2, i], there)], got.at[2, i]))
+    quarter = half // 2
+    early, late = pl.ds(0, quarter), pl.ds(quarter, quarter)
+
+    def send(src, dst, dev):
+        return exchange([(src, dst, dev)], src)
+
+    def rows(i):
+        return pl.ds(pl.multiple_of(i * half, half), half)
+
+    fin[c] = take(3, c).astype(BF16)
+    to_up = send(fin.at[c], got.at[0, c], up)
+    others = [send(fin.at[c, early], got.at[1, c, early], down)]
+    keep(3, shared)
+    fin[1 - c] = take(3, 1 - c).astype(BF16)
+    to_down = send(fin.at[1 - c], got.at[1, 1 - c], down)
+    others.append(send(fin.at[c, late], got.at[1, c, late], down))
+    others.append(send(fin.at[1 - c], got.at[0, 1 - c], up))
+    for i in range(2):
+        drains.append(fetch(fin.at[i], upd_o.at[x, rows(i)]))
+    to_up.wait()
+    passed = [send(got.at[0, c], upd_o.at[after(n_leaf - 1), rows(c)], up)]
+    to_down.wait()
+    passed.append(send(got.at[1, 1 - c], upd_o.at[after(1), rows(1 - c)], down))
+    for arrival in others:
+        arrival.wait()
     for k, origin in ((0, after(n_leaf - 1)), (1, after(1))):
         for i in range(2):
-            drains.append(fetch(got.at[k, i], upd_o.at[origin, pl.ds(i * half, half)]))
-    for i, arrival in zip((c, 1 - c), passed):
-        arrival.wait()
-        drains.append(fetch(got.at[2, i], upd_o.at[after(2), pl.ds(pl.multiple_of(i * half, half), half)]))
+            drains.append(fetch(got.at[k, i], upd_o.at[origin, rows(i)]))
+    for arrival in passed:
+        arrival.wait()
     for copy in drains:
         copy.wait()
 
@@ -475,14 +496,14 @@
         pltpu.VMEM((2, wide, wide), BF16),
         pltpu.VMEM((2, wide, wide), BF16),
         pltpu.VMEM((tiles, rhs, wide), F32),
-        pltpu.VMEM((levels, rhs, wide), F32),
+        [pltpu.VMEM((levels - 1, wide, wide), BF16)] * 2,
         pltpu.VMEM((levels, nc, nz, part, wide), BF16),
         [pltpu.VMEM((tiles, wide, wide), BF16)] * 2,
         pltpu.VMEM((2, wide, wide), BF16),
         pltpu.VMEM((2, mid, wide), F32),
         pltpu.VMEM((tiles, rhs, wide), BF16),
         [[pltpu.VMEM((2, length // 2, wide), BF16)] * 4 for length in (wide, wide, rhs)]
-        + [[pltpu.VMEM((2, rhs // 2, wide), BF16), pltpu.VMEM((n_leaf - 1, 2, rhs // 2, wide), BF16)]],
+        + [[pltpu.VMEM((2, rhs // 2, wide), BF16), pltpu.VMEM((2, 2, rhs // 2, wide), BF16)]],
         slices,
         floods,
         pub,

time: 82 us -> 76.1 us (0.928)
  Pallas kernels: 81 us -> 75.3 us
    pallas_call x1, Pallas kernels: 78.6 us -> 72.9 us  [on_device(): pl.pallas_call(functools.partial(kernel, grid, n_leaf), out_shape=(jax.Sh...]
where the time goes in v6:
time: 76.1 us; the launch traced here: 75.9 us
  Pallas kernels  75.3 us (99%)
    pallas_call x1, Pallas kernels, on_device(): pl.pallas_call(functools.partial(kernel, grid, n_leaf), out_shape=(jax.Sh...  72.9 us
    pallas_call x1, Pallas kernels, on_device(): pl.pallas_call(settle, out_shape=tuple((jax.ShapeDtypeStruct(shape, BF16)...  2.4 us

profile of v6, /device:TPU:1, one launch (start us, length us, event | category | flops | bytes accessed | tf_op | source)
XLA Modules:
  0.0 75.9 jit_solution(15011217778505372248)
XLA Ops:
  0.6 72.9 %shard_map.86 = (bf16[4,2,8,16,512]{4,3,2,1,0:T(8,128)(2,1)}, bf16[4,256,512]{2,1,0:T(8,128)(2,1)}) custom-call(s32[4]{0:T(128)} %sup.1, s32[4,1,4]{2,1,0:T(1,128)} %cnt.1, bf16[1,4,256,512]{3,2,1,0:T(8,128)(2,1)} %rs_h.1, bf16[4,1,4,512,512]{4,3,2,1,0:T(8,128)(2,1)} %pan_h.1, bf16[1,512,512]{2,1,0:T(8,128)(2,1)} %dl_h.1, bf16[2,512,512]{2,1,0:T(8,128)(2,1)} %dp_h.1, ...), custom_call_target="tpu_custom_call" | custom-call | tf_op jit(solution)/shard_map/pallas_call | solution.py:513
  73.5 2.4 %shard_map.87 = (bf16[4,2,8,16,512]{4,3,2,1,0:T(8,128)(2,1)}, bf16[4,256,512]{2,1,0:T(8,128)(2,1)}) custom-call(bf16[4,2,8,16,512]{4,3,2,1,0:T(8,128)(2,1)} %get-tuple-element.6.solved_h, bf16[4,256,512]{2,1,0:T(8,128)(2,1)} %get-tuple-element.7.updated_h), custom_call_target="tpu_custom_call" | custom-call | tf_op jit(solution)/shard_map/pallas_call | solution.py:527

commit v7 on v6

--- a/solution.py
+++ b/solution.py
@@ -338,10 +338,11 @@
     for m in (1, 2, 3):
         prepare(m)
         arrivals[m] = begin(m)
+    pub_a = publish_y(0, pub_a)
     coupled = first_core()
     arrival = flood(0, rows_of(0, arrival))
-    pub_a = publish_y(0, pub_a)
     pub_b = publish_y(1, pub_b)
+    pub_a = publish_z(0, pub_a)
     mask_tiles(2)
     relayed3.wait()
     last3 = fold_on(live[1], folds[1])
@@ -350,18 +351,19 @@
     coupled.wait()
     for m in range(1, levels):
         first[1][m - 1] = first[0][m - 1] + first[1][m - 1]
-    pub_a = publish_z(0, pub_a)
+    pub_a = publish_gather(0, pub_a)
     shared0 = share(0, arrival)
     arrivals[1] = slice_z(1, arrivals[1])
-    pub_a = publish_gather(0, pub_a)
     arrivals[2] = columns_y(2, arrivals[2])
     pub_b = publish_z(1, pub_b)
     arrivals[3] = columns_y(3, arrivals[3])
+    pub_a = publish_last(0, pub_a)
+    keep(0, shared0)
+    bulk(0)
     merge1 = flood(1, rows_of(1, arrivals[1]))
     for m in (2, 3):
         arrivals[m] = rows_z(m, arrivals[m])
     direct2 = fold_near(live[0], folds[0])
-    pub_a = publish_last(0, pub_a)
     pub_b = publish_gather(1, pub_b)
     solved1, spread1 = solve(1, merge1)
     pub_a.wait()
@@ -370,9 +372,6 @@
     relayed2.wait()
     last2 = fold_on(live[0], folds[0])
     pub_b = publish_last(1, pub_b)
-    keep(0, shared0)
-    bulk(0)
-    sum_tiles(3, (direct3, last3))
     piece = piece_of(3, arrivals[3])
     pub_b.wait()
     piece = piece - jnp.dot(solved1, coupling(1, 3), preferred_element_type=F32)
@@ -399,6 +398,7 @@
         last.append(fold_on(upd, folds[2], i, 2))
     shared = share(2, spread2)
     sum_tiles(2, (direct2, last2))
+    sum_tiles(3, (direct3, last3))
     keep(2, shared)
     for arrival in (direct, *last):
         arrival.wait()

time: 76.1 us -> 76.1 us (level)
  no operation moved by 1% of the time
where the time goes in v7:
time: 76.1 us; the launch traced here: 76 us
  Pallas kernels  75.3 us (99%)
    pallas_call x1, Pallas kernels, on_device(): pl.pallas_call(functools.partial(kernel, grid, n_leaf), out_shape=(jax.Sh...  73 us
    pallas_call x1, Pallas kernels, on_device(): pl.pallas_call(settle, out_shape=tuple((jax.ShapeDtypeStruct(shape, BF16)...  2.4 us

profile of v7, /device:TPU:1, one launch (start us, length us, event | category | flops | bytes accessed | tf_op | source)
XLA Modules:
  0.0 76.0 jit_solution(3686589838670624490)
XLA Ops:
  0.6 73.0 %shard_map.86 = (bf16[4,2,8,16,512]{4,3,2,1,0:T(8,128)(2,1)}, bf16[4,256,512]{2,1,0:T(8,128)(2,1)}) custom-call(s32[4]{0:T(128)} %sup.1, s32[4,1,4]{2,1,0:T(1,128)} %cnt.1, bf16[1,4,256,512]{3,2,1,0:T(8,128)(2,1)} %rs_h.1, bf16[4,1,4,512,512]{4,3,2,1,0:T(8,128)(2,1)} %pan_h.1, bf16[1,512,512]{2,1,0:T(8,128)(2,1)} %dl_h.1, bf16[2,512,512]{2,1,0:T(8,128)(2,1)} %dp_h.1, ...), custom_call_target="tpu_custom_call" | custom-call | tf_op jit(solution)/shard_map/pallas_call | solution.py:513
  73.6 2.4 %shard_map.87 = (bf16[4,2,8,16,512]{4,3,2,1,0:T(8,128)(2,1)}, bf16[4,256,512]{2,1,0:T(8,128)(2,1)}) custom-call(bf16[4,2,8,16,512]{4,3,2,1,0:T(8,128)(2,1)} %get-tuple-element.6.solved_h, bf16[4,256,512]{2,1,0:T(8,128)(2,1)} %get-tuple-element.7.updated_h), custom_call_target="tpu_custom_call" | custom-call | tf_op jit(solution)/shard_map/pallas_call | solution.py:527

commit v8 on v7

--- a/solution.py
+++ b/solution.py
@@ -167,6 +167,7 @@
         n = meeting(m, n_leaf)
         cs, cr = floods[m]
         own = (x % n) * ny + y
+        value = value.astype(BF16)
         cs[...] = value
         cr[own] = value
         return exchange(
@@ -186,9 +187,9 @@
         else:
             parts = []
             for k in range(ny):
-                value = cr[k]
+                value = cr[k].astype(F32)
                 for a in range(1, n):
-                    value = value + cr[a * ny + k]
+                    value = value + cr[a * ny + k].astype(F32)
                 parts.append(value.astype(BF16))
             merged = jnp.concatenate(parts, axis=1)
         need(("d0", "d1", "d2", "d2")[m])
@@ -475,8 +476,8 @@
         slices.append([pltpu.VMEM((nc, mid, wide), BF16), pltpu.VMEM((mid, wide), BF16)])
         for (ways, rows), length in spread:
             slices[m] += [pltpu.VMEM((ways, rows, length), BF16), pltpu.VMEM((ways - 1, rows, length), BF16)]
-        piece, kind = ((part, wide), BF16) if m < 2 else ((part, low), F32)
-        floods.append([pltpu.VMEM(piece, kind), pltpu.VMEM((meeting(m, n_leaf) * ny, *piece), kind)])
+        piece = (part, wide) if m < 2 else (part, low)
+        floods.append([pltpu.VMEM(piece, BF16), pltpu.VMEM((meeting(m, n_leaf) * ny, *piece), BF16)])
     pub = [
         [
             pltpu.VMEM((nc, pairs, wide // nc, wide), BF16),

time: 76.1 us -> 75 us (0.986)
  Pallas kernels: 75.3 us -> 74.2 us
    pallas_call x1, Pallas kernels: 73 us -> 71.8 us  [on_device(): pl.pallas_call(functools.partial(kernel, grid, n_leaf), out_shape=(jax.Sh...]
where the time goes in v8:
time: 75 us; the launch traced here: 74.8 us
  Pallas kernels  74.2 us (99%)
    pallas_call x1, Pallas kernels, on_device(): pl.pallas_call(functools.partial(kernel, grid, n_leaf), out_shape=(jax.Sh...  71.8 us
    pallas_call x1, Pallas kernels, on_device(): pl.pallas_call(settle, out_shape=tuple((jax.ShapeDtypeStruct(shape, BF16)...  2.4 us

profile of v8, /device:TPU:1, one launch (start us, length us, event | category | flops | bytes accessed | tf_op | source)
XLA Modules:
  0.0 74.8 jit_solution(342147484981432549)
XLA Ops:
  0.6 71.8 %shard_map.86 = (bf16[4,2,8,16,512]{4,3,2,1,0:T(8,128)(2,1)}, bf16[4,256,512]{2,1,0:T(8,128)(2,1)}) custom-call(s32[4]{0:T(128)} %sup.1, s32[4,1,4]{2,1,0:T(1,128)} %cnt.1, bf16[1,4,256,512]{3,2,1,0:T(8,128)(2,1)} %rs_h.1, bf16[4,1,4,512,512]{4,3,2,1,0:T(8,128)(2,1)} %pan_h.1, bf16[1,512,512]{2,1,0:T(8,128)(2,1)} %dl_h.1, bf16[2,512,512]{2,1,0:T(8,128)(2,1)} %dp_h.1, ...), custom_call_target="tpu_custom_call" | custom-call | tf_op jit(solution)/shard_map/pallas_call | solution.py:514
  72.4 2.4 %shard_map.87 = (bf16[4,2,8,16,512]{4,3,2,1,0:T(8,128)(2,1)}, bf16[4,256,512]{2,1,0:T(8,128)(2,1)}) custom-call(bf16[4,2,8,16,512]{4,3,2,1,0:T(8,128)(2,1)} %get-tuple-element.6.solved_h, bf16[4,256,512]{2,1,0:T(8,128)(2,1)} %get-tuple-element.7.updated_h), custom_call_target="tpu_custom_call" | custom-call | tf_op jit(solution)/shard_map/pallas_call | solution.py:528
